TPU v7x, 1024 devices: a whole 4x8x16 slice. The times are simulated.
1024 devices in a mesh: band: 64 (over x, z), mem: 16 (over y, core).
Axes of the slice: x: 4, y: 8, z: 16, core: 2. Of those that a mesh axis runs over, the one named last changes fastest.
Arguments:
- state: float32 [1024, 512, 256], P('mem', 'band'), may hold values from -6 to 6
- courant: float32 [2, 512, 256], P(None, 'band'), may hold values from 0.15 to 0.4
- obs_pert: bfloat16 [64, 512, 1024], P('band'), may hold values from -8 to 8
- obs_cell: int32 [64, 512], P('band'), may hold values from 0 to 131071, as said below
- block_rows: int32 [64], replicated, may hold values from 64 to 512, as said below
- band_list: int32 [64, 2], P('band'), may hold values from 0 to 63, as said below
Outputs:
- analysis: float32 [1024, 512, 256], P('mem', 'band')
Inputs may be any that keep to these rules, and one draw needn't show every extreme that they name: `band_list`: row b holds 2 different block numbers, each one of b - 1, b, b + 1 taken modulo 64. `block_rows`: the first that many rows of a block are live. Some block has exactly 512 in every draw. `obs_cell`: the rows of block j lie in latitude rows j * 8 to (j + 1) * 8 - 1; a cell is numbered latitude row times 256 plus longitude.
All inputs are finite; a program needn't handle non-finite values.
Results may differ from a plain program's by a relative error of at most 0.0045.
Values may be sent and summed in bfloat16 or wider, within the bound.
No kernel may reach another device: no remote copies, remote signals or barrier semaphores. Data moves between devices by JAX's collectives and lax.ppermute only.
A program may use at most 32 MiB of HBM per device.

v0:
```python
import jax
import jax.numpy as jnp
from jax import lax
from jax.sharding import PartitionSpec as P

STEPS = 6
LIST = 2
DEGREE = 4


DIFFUSION = 0.05
COEFFS = (1.0, -0.5, 0.375, -0.3125, 0.2734375)


def padded_2(cells, sides, width):
    for axis, dim in sides:
        count = lax.axis_size(axis)
        head = lax.slice_in_dim(cells, 0, width, axis=dim)
        tail = lax.slice_in_dim(cells, cells.shape[dim] - width, cells.shape[dim], axis=dim)
        cells = jnp.concatenate(
            [
                lax.ppermute(tail, axis, [(i, (i + 1) % count) for i in range(count)]),
                cells,
                lax.ppermute(head, axis, [((i + 1) % count, i) for i in range(count)]),
            ],
            axis=dim,
        )
    return cells


def advance(padded, winds):
    centre = padded[:, 1:-1]
    northern = padded[:, :-2]
    southern = padded[:, 2:]
    western = jnp.roll(centre, 1, axis=2)
    eastern = jnp.roll(centre, -1, axis=2)
    saturation = 0.5 + 0.5 * jnp.tanh(centre)
    return (
        centre
        - winds[0][None] * saturation * (centre - northern)
        - winds[1][None] * saturation * (centre - western)
        + DIFFUSION * (northern + southern + eastern + western - 4.0 * centre)
    )


def localization(obs_cells, live_rows, cell_flat, lat_count, lon_count, rows_band, gscale):
    obs_lat = obs_cells // lon_count
    obs_lon = obs_cells % lon_count
    cell_lat = cell_flat // lon_count
    cell_lon = cell_flat % lon_count
    lat_gap = jnp.abs(obs_lat[:, None] - cell_lat[None, :])
    lat_gap = jnp.minimum(lat_gap, lat_count - lat_gap)
    lon_gap = jnp.abs(obs_lon[:, None] - cell_lon[None, :])
    lon_gap = jnp.minimum(lon_gap, lon_count - lon_gap)
    lat_term = lat_gap.astype(jnp.float32) * (1.0 / rows_band)
    lon_term = lon_gap.astype(jnp.float32) * (4.0 / lon_count)
    decay = jnp.exp(-0.5 * (lat_term * lat_term + lon_term * lon_term)) * gscale
    return jnp.where(live_rows[:, None], decay, jnp.zeros_like(decay))


def transform(pert, observed, weight):
    series = pert
    combined = COEFFS[0] * pert
    for power in range(1, DEGREE + 1):
        projected = jnp.dot(
            observed, series.astype(jnp.bfloat16), preferred_element_type=jnp.float32
        )
        scaled = (projected * weight).astype(jnp.bfloat16)
        series = lax.dot_general(
            observed, scaled, (((0,), (0,)), ((), ())), preferred_element_type=jnp.float32
        )
        combined = combined + COEFFS[power] * series
    return combined


def shards(state, courant, obs_pert, obs_cell, block_rows, band_list):
    member_count, band_rows, lon_count = state.shape
    tracer = state
    for section in range(STEPS):
        padded = padded_2(tracer, (("band", 1),), 1)
        tracer = advance(padded, courant)
    band_cells = band_rows * lon_count
    columns = lax.all_to_all(
        tracer.reshape(member_count, band_cells), "mem", split_axis=1, concat_axis=0, tiled=True
    )
    members, group_cells = columns.shape
    average = jnp.mean(columns, axis=0, keepdims=True)
    pert = columns - average
    band_index = lax.axis_index("band")
    band_total = lax.axis_size("band")
    mem_index = lax.axis_index("mem")
    block_ids = band_list[0]
    offsets = (block_ids - band_index + 1) % band_total
    near_pert, near_cells = (
        padded_2(obs_pert, (("band", 0),), 1),
        padded_2(obs_cell, (("band", 0),), 1),
    )
    chosen = jnp.stack(
        [
            lax.dynamic_index_in_dim(near_pert, offsets[position], 0, keepdims=False)
            for position in range(LIST)
        ]
    )
    chosen_cells = jnp.stack(
        [
            lax.dynamic_index_in_dim(near_cells, offsets[position], 0, keepdims=False)
            for position in range(LIST)
        ]
    )
    block_count = block_rows.shape[0]
    matches = jnp.arange(block_count, dtype=jnp.int32)[None, :] == block_ids[:, None]
    counts = jnp.sum(
        jnp.where(matches, block_rows[None, :], jnp.zeros_like(block_rows)[None, :]), axis=1
    )
    obs_rows = chosen.shape[1]
    live_rows = (jnp.arange(obs_rows, dtype=jnp.int32)[None, :] < counts[:, None]).reshape(-1)
    observed = chosen.reshape(LIST * obs_rows, members)
    cell_flat = (
        band_index * band_cells + mem_index * group_cells + jnp.arange(group_cells, dtype=jnp.int32)
    )
    gscale = 1.0 / (members + LIST * obs_rows)
    weight = localization(
        chosen_cells.reshape(-1),
        live_rows,
        cell_flat,
        band_rows * band_total,
        lon_count,
        band_rows,
        gscale,
    )
    analysed = average + transform(pert, observed, weight)
    returned = lax.all_to_all(analysed, "mem", split_axis=0, concat_axis=1, tiled=True)
    return returned.reshape(member_count, band_rows, lon_count)


def solution(mesh):
    return jax.shard_map(
        shards,
        mesh=mesh,
        in_specs=(
            P("mem", "band", None),
            P(None, "band", None),
            P("band", None, None),
            P("band", None),
            P(),
            P("band", None),
        ),
        out_specs=P("mem", "band", None),
        check_vma=False,
    )
```

profile of v0, /device:TPU:1, one launch (start us, length us, event | category | flops | bytes accessed | tf_op | source)
XLA Modules:
  0.0 182.8 jit_solution(15520735191842912971)
XLA Ops:
  0.0 5.0 %collective-permute-start.12 = (bf16[1,512,1024]{2,1,0:T(8,128)(2,1)}, bf16[1,512,1024]{2,1,0:T(8,128)(2,1)}, u32[]{:S(2)}, u32[]{:S(2)}) collective-permute-start(bf16[1,512,1024]{2,1,0:T(8,128)(2,1)} %param.8), channel_id=1, source_target_pairs={{0,16},{16,32},{32,48},{48,64},{64,80},{80,96},{96,112},{112,128},... | collective-permute-start | bytes 3145736 | tf_op jit(solution)/shard_map/ppermute | solution.py:22
  5.0 18.1 %collective-permute-start.13 = (bf16[1,512,1024]{2,1,0:T(8,128)(2,1)}, bf16[1,512,1024]{2,1,0:T(8,128)(2,1)S(1)}, u32[]{:S(2)}, u32[]{:S(2)}) collective-permute-start(bf16[1,512,1024]{2,1,0:T(8,128)(2,1)} %param.8), channel_id=1, source_target_pairs={{16,0},{32,16},{48,32},{64,48},{80,64},{96,80},{112,96},{128,112},... | collective-permute-start | bytes 3145736 | tf_op jit(solution)/shard_map/ppermute | solution.py:24
  23.1 3.4 %collective-permute-start.15 = (s32[1,512]{1,0:T(1,128)}, s32[1,512]{1,0:T(1,128)S(1)}, u32[]{:S(2)}, u32[]{:S(2)}) collective-permute-start(s32[1,512]{1,0:T(1,128)} %param.9), channel_id=1, source_target_pairs={{16,0},{32,16},{48,32},{64,48},{80,64},{96,80},{112,96},{128,112},... | collective-permute-start | bytes 6152 | tf_op jit(solution)/shard_map/ppermute | solution.py:24
  26.4 1.9 %collective-permute-start.14 = (s32[1,512]{1,0:T(1,128)}, s32[1,512]{1,0:T(1,128)S(1)}, u32[]{:S(2)}, u32[]{:S(2)}) collective-permute-start(s32[1,512]{1,0:T(1,128)} %param.9), channel_id=1, source_target_pairs={{0,16},{16,32},{32,48},{48,64},{64,80},{80,96},{96,112},{112,128},... | collective-permute-start | bytes 6152 | tf_op jit(solution)/shard_map/ppermute | solution.py:22
  29.7 6.7 %collective-permute-start.1 = (f32[64,1,256]{2,1,0:T(1,128)S(1)}, f32[64,1,256]{2,1,0:T(1,128)S(1)}, u32[]{:S(2)}, u32[]{:S(2)}) collective-permute-start(f32[64,1,256]{2,1,0:T(1,128)S(1)} %get-tuple-element.42), channel_id=1, source_target_pairs={{16,0},{32,16},{48,32},{64,48},{80,64},{96,80},{112,96},{128,112},... | collective-permute-start | bytes 196616 | tf_op jit(solution)/shard_map/ppermute | solution.py:24
  37.5 1.4 fusion.142
  43.7 1.5 collective-permute-done.15
  45.2 1.9 %collective-permute-start = (f32[64,1,256]{2,1,0:T(1,128)S(1)}, f32[64,1,256]{2,1,0:T(1,128)S(1)}, u32[]{:S(2)}, u32[]{:S(2)}) collective-permute-start(f32[64,1,256]{2,1,0:T(1,128)S(1)} %get-tuple-element.41), channel_id=1, source_target_pairs={{0,16},{16,32},{32,48},{48,64},{64,80},{80,96},{96,112},{112,128},... | collective-permute-start | bytes 196616 | tf_op jit(solution)/shard_map/ppermute | solution.py:22
  47.2 7.0 %collective-permute-done = f32[64,1,256]{2,1,0:T(1,128)S(1)} collective-permute-done((f32[64,1,256]{2,1,0:T(1,128)S(1)}, f32[64,1,256]{2,1,0:T(1,128)S(1)}, u32[]{:S(2)}, u32[]{:S(2)}) %collective-permute-start) | collective-permute-done | bytes 65568 | tf_op jit(solution)/shard_map/ppermute | solution.py:22
  55.1 3.4 %collective-permute-start.3 = (f32[64,1,256]{2,1,0:T(1,128)S(1)}, f32[64,1,256]{2,1,0:T(1,128)S(1)}, u32[]{:S(2)}, u32[]{:S(2)}) collective-permute-start(f32[64,1,256]{2,1,0:T(1,128)S(1)} %get-tuple-element.36), channel_id=1, source_target_pairs={{16,0},{32,16},{48,32},{64,48},{80,64},{96,80},{112,96},{128,112},... | collective-permute-start | bytes 196616 | tf_op jit(solution)/shard_map/ppermute | solution.py:24
  58.4 1.9 %collective-permute-start.2 = (f32[64,1,256]{2,1,0:T(1,128)S(1)}, f32[64,1,256]{2,1,0:T(1,128)S(1)}, u32[]{:S(2)}, u32[]{:S(2)}) collective-permute-start(f32[64,1,256]{2,1,0:T(1,128)S(1)} %get-tuple-element.35), channel_id=1, source_target_pairs={{0,16},{16,32},{32,48},{48,64},{64,80},{80,96},{96,112},{112,128},... | collective-permute-start | bytes 196616 | tf_op jit(solution)/shard_map/ppermute | solution.py:22
  60.5 6.3 %collective-permute-done.2 = f32[64,1,256]{2,1,0:T(1,128)S(1)} collective-permute-done((f32[64,1,256]{2,1,0:T(1,128)S(1)}, f32[64,1,256]{2,1,0:T(1,128)S(1)}, u32[]{:S(2)}, u32[]{:S(2)}) %collective-permute-start.2) | collective-permute-done | bytes 65568 | tf_op jit(solution)/shard_map/ppermute | solution.py:22
  67.7 1.9 %collective-permute-start.5 = (f32[64,1,256]{2,1,0:T(1,128)S(1)}, f32[64,1,256]{2,1,0:T(1,128)S(1)}, u32[]{:S(2)}, u32[]{:S(2)}) collective-permute-start(f32[64,1,256]{2,1,0:T(1,128)S(1)} %get-tuple-element.30), channel_id=1, source_target_pairs={{16,0},{32,16},{48,32},{64,48},{80,64},{96,80},{112,96},{128,112},... | collective-permute-start | bytes 196616 | tf_op jit(solution)/shard_map/ppermute | solution.py:24
  69.6 3.4 %collective-permute-start.4 = (f32[64,1,256]{2,1,0:T(1,128)S(1)}, f32[64,1,256]{2,1,0:T(1,128)S(1)}, u32[]{:S(2)}, u32[]{:S(2)}) collective-permute-start(f32[64,1,256]{2,1,0:T(1,128)S(1)} %get-tuple-element.29), channel_id=1, source_target_pairs={{0,16},{16,32},{32,48},{48,64},{64,80},{80,96},{96,112},{112,128},... | collective-permute-start | bytes 196616 | tf_op jit(solution)/shard_map/ppermute | solution.py:22
  73.1 4.8 %collective-permute-done.4 = f32[64,1,256]{2,1,0:T(1,128)S(1)} collective-permute-done((f32[64,1,256]{2,1,0:T(1,128)S(1)}, f32[64,1,256]{2,1,0:T(1,128)S(1)}, u32[]{:S(2)}, u32[]{:S(2)}) %collective-permute-start.4) | collective-permute-done | bytes 65568 | tf_op jit(solution)/shard_map/ppermute | solution.py:22
  78.8 1.9 %collective-permute-start.7 = (f32[64,1,256]{2,1,0:T(1,128)S(1)}, f32[64,1,256]{2,1,0:T(1,128)S(1)}, u32[]{:S(2)}, u32[]{:S(2)}) collective-permute-start(f32[64,1,256]{2,1,0:T(1,128)S(1)} %get-tuple-element.24), channel_id=1, source_target_pairs={{16,0},{32,16},{48,32},{64,48},{80,64},{96,80},{112,96},{128,112},... | collective-permute-start | bytes 196616 | tf_op jit(solution)/shard_map/ppermute | solution.py:24
  80.7 3.4 %collective-permute-start.6 = (f32[64,1,256]{2,1,0:T(1,128)S(1)}, f32[64,1,256]{2,1,0:T(1,128)S(1)}, u32[]{:S(2)}, u32[]{:S(2)}) collective-permute-start(f32[64,1,256]{2,1,0:T(1,128)S(1)} %get-tuple-element.23), channel_id=1, source_target_pairs={{0,16},{16,32},{32,48},{48,64},{64,80},{80,96},{96,112},{112,128},... | collective-permute-start | bytes 196616 | tf_op jit(solution)/shard_map/ppermute | solution.py:22
  84.2 4.8 %collective-permute-done.6 = f32[64,1,256]{2,1,0:T(1,128)S(1)} collective-permute-done((f32[64,1,256]{2,1,0:T(1,128)S(1)}, f32[64,1,256]{2,1,0:T(1,128)S(1)}, u32[]{:S(2)}, u32[]{:S(2)}) %collective-permute-start.6) | collective-permute-done | bytes 65568 | tf_op jit(solution)/shard_map/ppermute | solution.py:22
  89.9 1.9 %collective-permute-start.9 = (f32[64,1,256]{2,1,0:T(1,128)S(1)}, f32[64,1,256]{2,1,0:T(1,128)S(1)}, u32[]{:S(2)}, u32[]{:S(2)}) collective-permute-start(f32[64,1,256]{2,1,0:T(1,128)S(1)} %get-tuple-element.18), channel_id=1, source_target_pairs={{16,0},{32,16},{48,32},{64,48},{80,64},{96,80},{112,96},{128,112},... | collective-permute-start | bytes 196616 | tf_op jit(solution)/shard_map/ppermute | solution.py:24
  91.9 3.4 %collective-permute-start.8 = (f32[64,1,256]{2,1,0:T(1,128)S(1)}, f32[64,1,256]{2,1,0:T(1,128)S(1)}, u32[]{:S(2)}, u32[]{:S(2)}) collective-permute-start(f32[64,1,256]{2,1,0:T(1,128)S(1)} %get-tuple-element.17), channel_id=1, source_target_pairs={{0,16},{16,32},{32,48},{48,64},{64,80},{80,96},{96,112},{112,128},... | collective-permute-start | bytes 196616 | tf_op jit(solution)/shard_map/ppermute | solution.py:22
  95.4 4.8 %collective-permute-done.8 = f32[64,1,256]{2,1,0:T(1,128)S(1)} collective-permute-done((f32[64,1,256]{2,1,0:T(1,128)S(1)}, f32[64,1,256]{2,1,0:T(1,128)S(1)}, u32[]{:S(2)}, u32[]{:S(2)}) %collective-permute-start.8) | collective-permute-done | bytes 65568 | tf_op jit(solution)/shard_map/ppermute | solution.py:22
  100.9 1.9 %collective-permute-start.11 = (f32[64,1,256]{2,1,0:T(1,128)S(1)}, f32[64,1,256]{2,1,0:T(1,128)S(1)}, u32[]{:S(2)}, u32[]{:S(2)}) collective-permute-start(f32[64,1,256]{2,1,0:T(1,128)S(1)} %get-tuple-element.12), channel_id=1, source_target_pairs={{16,0},{32,16},{48,32},{64,48},{80,64},{96,80},{112,96},{128,112},... | collective-permute-start | bytes 196616 | tf_op jit(solution)/shard_map/ppermute | solution.py:24
  102.8 3.4 %collective-permute-start.10 = (f32[64,1,256]{2,1,0:T(1,128)S(1)}, f32[64,1,256]{2,1,0:T(1,128)S(1)}, u32[]{:S(2)}, u32[]{:S(2)}) collective-permute-start(f32[64,1,256]{2,1,0:T(1,128)S(1)} %get-tuple-element.11), channel_id=1, source_target_pairs={{0,16},{16,32},{32,48},{48,64},{64,80},{80,96},{96,112},{112,128},... | collective-permute-start | bytes 196616 | tf_op jit(solution)/shard_map/ppermute | solution.py:22
  106.5 4.6 %collective-permute-done.10 = f32[64,1,256]{2,1,0:T(1,128)S(1)} collective-permute-done((f32[64,1,256]{2,1,0:T(1,128)S(1)}, f32[64,1,256]{2,1,0:T(1,128)S(1)}, u32[]{:S(2)}, u32[]{:S(2)}) %collective-permute-start.10) | collective-permute-done | bytes 65568 | tf_op jit(solution)/shard_map/ppermute | solution.py:22
  112.7 16.5 %all-to-all-start = ((f32[64,16,128]{2,0,1:T(8,128)}), f32[64,16,128]{2,0,1:T(8,128)S(1)}, u32[]{:S(2)}, u32[]{:S(2)}) async-start(f32[64,16,128]{2,0,1:T(8,128)} %copy.9), calls=%async_computation | async-start | bytes 1048576 | tf_op jit(solution)/shard_map/all_to_all | solution.py:83
  129.3 1.3 constant_dynamic-update-slice_fusion.2
  131.2 15.3 %all-to-all-done = f32[64,16,128]{2,0,1:T(8,128)S(1)} async-done(((f32[64,16,128]{2,0,1:T(8,128)}), f32[64,16,128]{2,0,1:T(8,128)S(1)}, u32[]{:S(2)}, u32[]{:S(2)}) %all-to-all-start) | async-done | bytes 524320 | tf_op jit(solution)/shard_map/all_to_all | solution.py:83
  146.7 3.1 %fusion.8 = f32[1024,128]{1,0:T(8,128)} fusion(bf16[1024,1024]{1,0:T(8,128)(2,1)S(1)} %bitcast.38, bf16[1024,128]{1,0:T(8,128)(2,1)S(1)} %bitcast.44, s32[128]{0:T(128)S(1)} %get-tuple-element.53, s32[1024]{0:T(1024)S(1)} %get-tuple-element.48, s32[128]{0:T(128)S(1)} %get-tuple-element.54, s32[1024]{0:T(1024)S(1)} %get-tuple-element.47, ...), kind=kOutput, calls=%fused_computation.14 | convolution fusion | flops 539492352 | bytes 2893824 | tf_op jit(solution)/shard_map/dot_general | solution.py:69
  149.7 4.1 %fusion.7 = f32[1024,128]{1,0:T(8,128)} fusion(bf16[1024,1024]{1,0:T(8,128)(2,1)S(1)} %bitcast.39, f32[1024,128]{1,0:T(8,128)} %fusion.8, s32[128]{0:T(128)S(1)} %get-tuple-element.53, s32[1024]{0:T(1024)S(1)} %get-tuple-element.48, s32[128]{0:T(128)S(1)} %get-tuple-element.54, s32[1024]{0:T(1024)S(1)} %get-tuple-element.47, pred[1024]{0:T(1024)(128)(4,1)S(1)} %lt.54), kind=kOutput, calls=%fused_computation.13 | convolution fusion | flops 539623424 | bytes 3155968 | tf_op jit(solution)/shard_map/dot_general | solution.py:69
  153.8 4.5 %fusion.82 = (f32[1024,128]{1,0:T(8,128)}, bf16[1024,128]{1,0:T(8,128)(2,1)S(1)}) fusion(f32[64,16,128]{2,0,1:T(8,128)S(1)} %all-to-all-done, f32[1024,128]{1,0:T(8,128)} %fusion.7, f32[1024,128]{1,0:T(8,128)} %fusion.8, f32[128]{0:T(128)S(1)} %broadcast_multiply_fusion, bf16[1024,1024]{1,0:T(8,128)(2,1)S(1)} %bitcast.40, s32[128]{0:T(128)S(1)} %get-tuple-element.53, ...), kind=kOutput, calls=%fused_computation.109 | convolution fusion | flops 540672000 | bytes 4467200 | tf_op jit(solution)/shard_map/dot_general | solution.py:69
  158.3 3.3 %fusion.1 = f32[1024,128]{1,0:T(8,128)S(1)} fusion(f32[1024,128]{1,0:T(8,128)} %get-tuple-element.51, bf16[1024,1024]{1,0:T(8,128)(2,1)S(1)} %bitcast.41, bf16[1024,128]{1,0:T(8,128)(2,1)S(1)} %get-tuple-element.52, f32[128]{0:T(128)S(1)} %broadcast_multiply_fusion, s32[128]{0:T(128)S(1)} %get-tuple-element.53, s32[1024]{0:T(1024)S(1)} %get-tuple-element.48, ...), kind=kOutput, calls=%fused_computation.3 | convolution fusion | flops 539885568 | bytes 3418624 | tf_op jit(solution)/shard_map/dot_general | solution.py:69
  161.6 20.0 %all_to_all.35 = f32[16,64,128]{2,1,0:T(8,128)S(1)} all-to-all(f32[16,64,128]{2,1,0:T(8,128)S(1)} %bitcast.43), channel_id=1, replica_groups=mesh['band'=64,'mem'=16] {'mem'}, dimensions={0} | all-to-all | bytes 1048576 | tf_op jit(solution)/shard_map/all_to_all | solution.py:132
  (67 shorter events, 12.0 us)
Async XLA Ops:
  0.0 47.1 %copy-start.3 = (s32[1,512]{1,0:T(1,128)S(1)}, s32[1,512]{1,0:T(1,128)}, u32[]{:S(2)}) copy-start(s32[1,512]{1,0:T(1,128)} %param.9) | copy-start | bytes 6148
  0.0 54.2 %copy-start = (f32[64,8,256]{2,1,0:T(8,128)S(1)}, f32[64,8,256]{2,1,0:T(8,128)}, u32[]{:S(2)}) copy-start(f32[64,8,256]{2,1,0:T(8,128)} %param.6) | copy-start | bytes 1572868
  0.0 38.9 %copy-start.2 = (f32[2,8,256]{2,1,0:T(8,128)S(1)}, f32[2,8,256]{2,1,0:T(8,128)}, u32[]{:S(2)}) copy-start(f32[2,8,256]{2,1,0:T(8,128)} %param.7) | copy-start | bytes 49156
  0.0 38.9 %copy-start.4 = (s32[1,2]{1,0:T(1,128)S(1)}, s32[1,2]{1,0:T(1,128)}, u32[]{:S(2)}) copy-start(s32[1,2]{1,0:T(1,128)} %param.11) | copy-start | bytes 28
  0.0 39.6 %copy-start.5 = (s32[64]{0:T(128)S(1)}, s32[64]{0:T(128)}, u32[]{:S(2)}) copy-start(s32[64]{0:T(128)} %param.10) | copy-start | bytes 772
  0.0 129.3 %collective-permute-start.12 = (bf16[1,512,1024]{2,1,0:T(8,128)(2,1)}, bf16[1,512,1024]{2,1,0:T(8,128)(2,1)}, u32[]{:S(2)}, u32[]{:S(2)}) collective-permute-start(bf16[1,512,1024]{2,1,0:T(8,128)(2,1)} %param.8), channel_id=1, source_target_pairs={{0,16},{16,32},{32,48},{48,64},{64,80},{80,96},{96,112},{112,128},... | collective-permute-start | bytes 3145736 | tf_op jit(solution)/shard_map/ppermute | solution.py:22
  5.0 125.7 %collective-permute-start.13 = (bf16[1,512,1024]{2,1,0:T(8,128)(2,1)}, bf16[1,512,1024]{2,1,0:T(8,128)(2,1)S(1)}, u32[]{:S(2)}, u32[]{:S(2)}) collective-permute-start(bf16[1,512,1024]{2,1,0:T(8,128)(2,1)} %param.8), channel_id=1, source_target_pairs={{16,0},{32,16},{48,32},{64,48},{80,64},{96,80},{112,96},{128,112},... | collective-permute-start | bytes 3145736 | tf_op jit(solution)/shard_map/ppermute | solution.py:24
  23.1 22.1 %collective-permute-start.15 = (s32[1,512]{1,0:T(1,128)}, s32[1,512]{1,0:T(1,128)S(1)}, u32[]{:S(2)}, u32[]{:S(2)}) collective-permute-start(s32[1,512]{1,0:T(1,128)} %param.9), channel_id=1, source_target_pairs={{16,0},{32,16},{48,32},{64,48},{80,64},{96,80},{112,96},{128,112},... | collective-permute-start | bytes 6152 | tf_op jit(solution)/shard_map/ppermute | solution.py:24
  26.4 20.7 %collective-permute-start.14 = (s32[1,512]{1,0:T(1,128)}, s32[1,512]{1,0:T(1,128)S(1)}, u32[]{:S(2)}, u32[]{:S(2)}) collective-permute-start(s32[1,512]{1,0:T(1,128)} %param.9), channel_id=1, source_target_pairs={{0,16},{16,32},{32,48},{48,64},{64,80},{80,96},{96,112},{112,128},... | collective-permute-start | bytes 6152 | tf_op jit(solution)/shard_map/ppermute | solution.py:22
  29.7 17.5 %collective-permute-start.1 = (f32[64,1,256]{2,1,0:T(1,128)S(1)}, f32[64,1,256]{2,1,0:T(1,128)S(1)}, u32[]{:S(2)}, u32[]{:S(2)}) collective-permute-start(f32[64,1,256]{2,1,0:T(1,128)S(1)} %get-tuple-element.42), channel_id=1, source_target_pairs={{16,0},{32,16},{48,32},{64,48},{80,64},{96,80},{112,96},{128,112},... | collective-permute-start | bytes 196616 | tf_op jit(solution)/shard_map/ppermute | solution.py:24
  45.2 9.0 %collective-permute-start = (f32[64,1,256]{2,1,0:T(1,128)S(1)}, f32[64,1,256]{2,1,0:T(1,128)S(1)}, u32[]{:S(2)}, u32[]{:S(2)}) collective-permute-start(f32[64,1,256]{2,1,0:T(1,128)S(1)} %get-tuple-element.41), channel_id=1, source_target_pairs={{0,16},{16,32},{32,48},{48,64},{64,80},{80,96},{96,112},{112,128},... | collective-permute-start | bytes 196616 | tf_op jit(solution)/shard_map/ppermute | solution.py:22
  55.1 5.4 %collective-permute-start.3 = (f32[64,1,256]{2,1,0:T(1,128)S(1)}, f32[64,1,256]{2,1,0:T(1,128)S(1)}, u32[]{:S(2)}, u32[]{:S(2)}) collective-permute-start(f32[64,1,256]{2,1,0:T(1,128)S(1)} %get-tuple-element.36), channel_id=1, source_target_pairs={{16,0},{32,16},{48,32},{64,48},{80,64},{96,80},{112,96},{128,112},... | collective-permute-start | bytes 196616 | tf_op jit(solution)/shard_map/ppermute | solution.py:24
  58.4 8.3 %collective-permute-start.2 = (f32[64,1,256]{2,1,0:T(1,128)S(1)}, f32[64,1,256]{2,1,0:T(1,128)S(1)}, u32[]{:S(2)}, u32[]{:S(2)}) collective-permute-start(f32[64,1,256]{2,1,0:T(1,128)S(1)} %get-tuple-element.35), channel_id=1, source_target_pairs={{0,16},{16,32},{32,48},{48,64},{64,80},{80,96},{96,112},{112,128},... | collective-permute-start | bytes 196616 | tf_op jit(solution)/shard_map/ppermute | solution.py:22
  67.7 5.4 %collective-permute-start.5 = (f32[64,1,256]{2,1,0:T(1,128)S(1)}, f32[64,1,256]{2,1,0:T(1,128)S(1)}, u32[]{:S(2)}, u32[]{:S(2)}) collective-permute-start(f32[64,1,256]{2,1,0:T(1,128)S(1)} %get-tuple-element.30), channel_id=1, source_target_pairs={{16,0},{32,16},{48,32},{64,48},{80,64},{96,80},{112,96},{128,112},... | collective-permute-start | bytes 196616 | tf_op jit(solution)/shard_map/ppermute | solution.py:24
  69.6 8.3 %collective-permute-start.4 = (f32[64,1,256]{2,1,0:T(1,128)S(1)}, f32[64,1,256]{2,1,0:T(1,128)S(1)}, u32[]{:S(2)}, u32[]{:S(2)}) collective-permute-start(f32[64,1,256]{2,1,0:T(1,128)S(1)} %get-tuple-element.29), channel_id=1, source_target_pairs={{0,16},{16,32},{32,48},{48,64},{64,80},{80,96},{96,112},{112,128},... | collective-permute-start | bytes 196616 | tf_op jit(solution)/shard_map/ppermute | solution.py:22
  78.8 5.4 %collective-permute-start.7 = (f32[64,1,256]{2,1,0:T(1,128)S(1)}, f32[64,1,256]{2,1,0:T(1,128)S(1)}, u32[]{:S(2)}, u32[]{:S(2)}) collective-permute-start(f32[64,1,256]{2,1,0:T(1,128)S(1)} %get-tuple-element.24), channel_id=1, source_target_pairs={{16,0},{32,16},{48,32},{64,48},{80,64},{96,80},{112,96},{128,112},... | collective-permute-start | bytes 196616 | tf_op jit(solution)/shard_map/ppermute | solution.py:24
  80.7 8.3 %collective-permute-start.6 = (f32[64,1,256]{2,1,0:T(1,128)S(1)}, f32[64,1,256]{2,1,0:T(1,128)S(1)}, u32[]{:S(2)}, u32[]{:S(2)}) collective-permute-start(f32[64,1,256]{2,1,0:T(1,128)S(1)} %get-tuple-element.23), channel_id=1, source_target_pairs={{0,16},{16,32},{32,48},{48,64},{64,80},{80,96},{96,112},{112,128},... | collective-permute-start | bytes 196616 | tf_op jit(solution)/shard_map/ppermute | solution.py:22
  89.9 5.4 %collective-permute-start.9 = (f32[64,1,256]{2,1,0:T(1,128)S(1)}, f32[64,1,256]{2,1,0:T(1,128)S(1)}, u32[]{:S(2)}, u32[]{:S(2)}) collective-permute-start(f32[64,1,256]{2,1,0:T(1,128)S(1)} %get-tuple-element.18), channel_id=1, source_target_pairs={{16,0},{32,16},{48,32},{64,48},{80,64},{96,80},{112,96},{128,112},... | collective-permute-start | bytes 196616 | tf_op jit(solution)/shard_map/ppermute | solution.py:24
  91.9 8.3 %collective-permute-start.8 = (f32[64,1,256]{2,1,0:T(1,128)S(1)}, f32[64,1,256]{2,1,0:T(1,128)S(1)}, u32[]{:S(2)}, u32[]{:S(2)}) collective-permute-start(f32[64,1,256]{2,1,0:T(1,128)S(1)} %get-tuple-element.17), channel_id=1, source_target_pairs={{0,16},{16,32},{32,48},{48,64},{64,80},{80,96},{96,112},{112,128},... | collective-permute-start | bytes 196616 | tf_op jit(solution)/shard_map/ppermute | solution.py:22
  100.9 5.6 %collective-permute-start.11 = (f32[64,1,256]{2,1,0:T(1,128)S(1)}, f32[64,1,256]{2,1,0:T(1,128)S(1)}, u32[]{:S(2)}, u32[]{:S(2)}) collective-permute-start(f32[64,1,256]{2,1,0:T(1,128)S(1)} %get-tuple-element.12), channel_id=1, source_target_pairs={{16,0},{32,16},{48,32},{64,48},{80,64},{96,80},{112,96},{128,112},... | collective-permute-start | bytes 196616 | tf_op jit(solution)/shard_map/ppermute | solution.py:24
  102.8 8.3 %collective-permute-start.10 = (f32[64,1,256]{2,1,0:T(1,128)S(1)}, f32[64,1,256]{2,1,0:T(1,128)S(1)}, u32[]{:S(2)}, u32[]{:S(2)}) collective-permute-start(f32[64,1,256]{2,1,0:T(1,128)S(1)} %get-tuple-element.11), channel_id=1, source_target_pairs={{0,16},{16,32},{32,48},{48,64},{64,80},{80,96},{96,112},{112,128},... | collective-permute-start | bytes 196616 | tf_op jit(solution)/shard_map/ppermute | solution.py:22
  111.8 18.8 %copy-start.1 = (bf16[1,512,1024]{2,1,0:T(8,128)(2,1)S(1)}, bf16[1,512,1024]{2,1,0:T(8,128)(2,1)}, u32[]{:S(2)}) copy-start(bf16[1,512,1024]{2,1,0:T(8,128)(2,1)} %param.8) | copy-start | bytes 3145732
  112.7 33.7 %all-to-all-start = ((f32[64,16,128]{2,0,1:T(8,128)}), f32[64,16,128]{2,0,1:T(8,128)S(1)}, u32[]{:S(2)}, u32[]{:S(2)}) async-start(f32[64,16,128]{2,0,1:T(8,128)} %copy.9), calls=%async_computation | async-start | bytes 1048576 | tf_op jit(solution)/shard_map/all_to_all | solution.py:83
where the time goes:
time: 184 us; the launch traced here: 183 us
  starting transfers between devices  79.8 us (43%)
  waiting for transfers between devices  49.1 us (27%)
  blocking collectives  20 us (11%)
  matrix products  14.9 us (8%)
  local copies, waits for them, and re-layouts  10.4 us (6%)
  between operations  4.35 us (2%)
  other arithmetic  4.23 us (2%)
    ppermute x8, starting transfers between devices, padded_2(): lax.ppermute(head, axis, [((i + 1) % count, i) for i in range(count)])  39.1 us
    ppermute x8, waiting for transfers between devices, padded_2(): lax.ppermute(tail, axis, [(i, (i + 1) % count) for i in range(count)])  32.3 us
    ppermute x8, starting transfers between devices, padded_2(): lax.ppermute(tail, axis, [(i, (i + 1) % count) for i in range(count)])  24.2 us
    all_to_all x1, blocking collectives, shards(): lax.all_to_all(analysed, 'mem', split_axis=0, concat_axis=1, tiled=True)  20 us
    all_to_all x1, starting transfers between devices, shards(): lax.all_to_all(tracer.reshape(member_count, band_cells), 'mem', split_axi...  16.5 us
    all_to_all x1, waiting for transfers between devices, shards(): lax.all_to_all(tracer.reshape(member_count, band_cells), 'mem', split_axi...  15.3 us
    dot_general x4, matrix products, transform(): lax.dot_general(observed, scaled, (((0,), (0,)), ((), ())), preferred_ele...  14.9 us
    slice x12, local copies, waits for them, and re-layouts, advance(): western = jnp.roll(centre, 1, axis=2)  4.2 us
  transfers between devices with their start and end apart: 17, of which 8 were waited for; matrix products, arithmetic and copies ran while one was open for 7% of the time, Pallas kernels for 0%

commit v1 on v0

v1 whole, which is shorter than its diff:
```python
import functools

import jax
import jax.numpy as jnp
from jax import lax
from jax.experimental import pallas as pl
from jax.experimental.pallas import tpu as pltpu
from jax.sharding import PartitionSpec as P


STEPS = 6
LIST = 2
DEGREE = 4

DIFFUSION = 0.05
COEFFS = (1.0, -0.5, 0.375, -0.3125, 0.2734375)

F32 = jnp.float32
BF16 = jnp.bfloat16
VMEM = pl.BlockSpec(memory_space=pltpu.VMEM)
PARAMS = pltpu.CompilerParams(vmem_limit_bytes=16 << 20)
SMEM = pl.BlockSpec(memory_space=pltpu.SMEM)
ANY = pl.BlockSpec(memory_space=pl.ANY)

EXTRA = 8
LANES = 128


def in_vmem(x):
    return pltpu.with_memory_space_constraint(x, pltpu.VMEM)


def pack(members, rows, state_ref, courant_ref, cells_ref, towards_a_ref, towards_b_ref, fields_ref):
    even = lax.rem(lax.axis_index("band"), 2) == 0
    lon = fields_ref.shape[2]
    sides = lon // LANES
    for row in range(rows):
        for side in range(sides):
            fields_ref[row, :, side * LANES : (side + 1) * LANES] = state_ref[
                pl.ds(side * rows + row, members, stride=sides * rows), :
            ]
    place = lax.broadcasted_iota(jnp.int32, (EXTRA, lon), 0)
    cells = cells_ref[...]
    lat = jnp.bitwise_and(lax.shift_right_logical(cells, 8), rows - 1).astype(F32)
    east = jnp.bitwise_and(cells, lon - 1).astype(F32)
    obs = jnp.zeros((EXTRA, lon), F32)
    for slot, values in ((4, lat[:, :lon]), (5, lat[:, lon:]), (6, east[:, :lon]), (7, east[:, lon:])):
        obs = jnp.where(place == slot, values, obs)
    for message_ref, from_tail in ((towards_a_ref, even), (towards_b_ref, jnp.logical_not(even))):
        first = jnp.where(from_tail, rows - STEPS, 0)
        for step in range(STEPS):
            message_ref[step, :members, :] = fields_ref[first + step].astype(BF16)
            extra = obs
            for wind in range(2):
                value = jnp.where(
                    from_tail,
                    courant_ref[wind, rows - STEPS + step : rows - STEPS + step + 1, :],
                    courant_ref[wind, step : step + 1, :],
                )
                high = value.astype(BF16).astype(F32)
                extra = jnp.where(place == wind, high, extra)
                extra = jnp.where(place == wind + 2, value - high, extra)
            message_ref[step, members:, :] = extra.astype(BF16)


def advect(members, rows, fields_ref, courant_ref, from_a_ref, from_b_ref, groups_ref, near_ref, held, winds):
    even = lax.rem(lax.axis_index("band"), 2) == 0
    lon = fields_ref.shape[2]
    total = rows + 2 * STEPS

    extra_a = from_a_ref[0, members:, :].astype(F32)
    extra_b = from_b_ref[0, members:, :].astype(F32)
    near_ref[0] = jnp.where(even, extra_b, extra_a)
    near_ref[1] = jnp.where(even, extra_a, extra_b)

    def keep(row, value0, value1):
        for wind, value in ((0, value0), (1, value1)):
            half = 0.5 * jnp.broadcast_to(value, (8, lon))
            winds[row, 2 * wind] = half
            winds[row, 2 * wind + 1] = half + DIFFUSION

    for message_ref, first in (
        (from_a_ref, jnp.where(even, STEPS + rows, 0)),
        (from_b_ref, jnp.where(even, 0, STEPS + rows)),
    ):
        for step in range(STEPS):
            held[first + step] = message_ref[step, :members, :].astype(F32)
            extra = message_ref[step, members:, :].astype(F32)
            keep(first + step, extra[0:1] + extra[2:3], extra[1:2] + extra[3:4])
    for row in range(rows):
        keep(STEPS + row, courant_ref[0, row : row + 1, :], courant_ref[1, row : row + 1, :])

    lane = lax.broadcasted_iota(jnp.int32, (8, LANES), 1)
    sides = lon // LANES

    def turned(parts, shift, edge):
        way = -1 if shift == 1 else 1
        mixed = [jnp.where(lane == edge, parts[(side + way) % sides], parts[side]) for side in range(sides)]
        return [pltpu.roll(part, shift % LANES, 1) for part in mixed]

    def group(index, carry):
        first = pl.multiple_of(index * 8, 8)

        def read(ref, row):
            return [ref[row, pl.ds(first, 8), side * LANES : (side + 1) * LANES] for side in range(sides)]

        def minus(left, right):
            return [x - y for x, y in zip(left, right)]

        values = [
            read(fields_ref, row - STEPS) if STEPS <= row < STEPS + rows else read(held, row) for row in range(total)
        ]
        for step in range(1, STEPS + 1):
            fresh = list(values)
            north = minus(values[step], values[step - 1])
            for row in range(step, total - step):
                centre = values[row]
                south = minus(values[row + 1], centre)
                west = minus(centre, turned(centre, 1, LANES - 1))
                east = turned(west, -1, 0)
                new = []
                for side in range(sides):
                    lanes = slice(side * LANES, (side + 1) * LANES)
                    curve = jnp.tanh(centre[side])
                    new.append(
                        centre[side]
                        - north[side] * (winds[row, 0, :, lanes] * curve + winds[row, 1, :, lanes])
                        - west[side] * (winds[row, 2, :, lanes] * curve + winds[row, 3, :, lanes])
                        + DIFFUSION * (south[side] + east[side])
                    )
                fresh[row] = new
                north = south
            values = fresh
        for row in range(rows):
            for side in range(sides):
                held[row, pl.ds(first, 8), side * LANES : (side + 1) * LANES] = values[STEPS + row][side]
        return carry

    lax.fori_loop(0, members // 8, group, 0)
    for row in range(rows):
        groups_ref[2 * row] = held[row, :, : lon // 2].astype(BF16)
        groups_ref[2 * row + 1] = held[row, :, lon // 2 :].astype(BF16)


def place_of(listed_ref, position):
    band, bands = lax.axis_index("band"), lax.axis_size("band")
    return lax.rem(listed_ref[0, position] - band + 1 + bands, bands)


def localize(rows, lon, gscale, listed_ref, counts_ref, cells_ref, near_ref, weight_ref):
    mem = lax.axis_index("mem")
    group_cells, obs_total = weight_ref.shape
    obs_rows = obs_total // LIST
    cells = cells_ref[...]
    own_lat = jnp.bitwise_and(lax.shift_right_logical(cells, 8), rows - 1).astype(F32)
    own_lon = jnp.bitwise_and(cells, lon - 1).astype(F32)

    def pair(side, slot):
        return jnp.concatenate([near_ref[side, slot : slot + 1, :], near_ref[side, slot + 1 : slot + 2, :]], axis=1)

    halves = lon // group_cells
    cell_row = (mem // halves).astype(F32)
    cell_lon = (
        lax.broadcasted_iota(jnp.int32, (group_cells, obs_rows), 0) + lax.rem(mem, halves) * group_cells
    ).astype(F32)
    lane = lax.broadcasted_iota(jnp.int32, (group_cells, obs_rows), 1)
    for position in range(LIST):
        place = place_of(listed_ref, position)
        lat = jnp.where(place == 0, pair(0, 4), jnp.where(place == 1, own_lat, pair(1, 4)))
        east = jnp.where(place == 0, pair(0, 6), jnp.where(place == 1, own_lon, pair(1, 6)))
        lat_gap = jnp.abs(lat + (place - 1).astype(F32) * rows - cell_row) * (1.0 / rows)
        lon_gap = jnp.abs(jnp.broadcast_to(east, cell_lon.shape) - cell_lon)
        lon_gap = jnp.minimum(lon_gap, lon - lon_gap) * (4.0 / lon)
        decay = jnp.exp(-0.5 * (jnp.broadcast_to(lat_gap * lat_gap, lon_gap.shape) + lon_gap * lon_gap)) * gscale
        live = lane < counts_ref[listed_ref[0, position]]
        weight_ref[:, position * obs_rows : (position + 1) * obs_rows] = jnp.where(live, decay, 0.0)


def transform(
    listed_ref, columns_ref, weight_hbm, own_ref, fetched_ref, swapped_ref, analysed_ref, observed_ref, weight_ref, sems
):
    shares, share, cells = columns_ref.shape
    obs_rows = own_ref.shape[1]
    first_core = lax.rem(lax.axis_index("mem"), 2) == 0
    copies = []
    for position in range(LIST):
        target = observed_ref.at[pl.ds(position * obs_rows, obs_rows), :]
        place = place_of(listed_ref, position)
        near = place != 1
        fetched = jnp.logical_and(near, (place == 0) == first_core)
        swapped = jnp.logical_and(near, (place == 0) != first_core)
        for chosen, source in ((place == 1, own_ref), (fetched, fetched_ref), (swapped, swapped_ref)):
            copy = pltpu.make_async_copy(source.at[0], target, sems.at[position])
            pl.when(chosen)(copy.start)
        copies.append(copy)
    weight_copy = pltpu.make_async_copy(weight_hbm, weight_ref, sems.at[LIST])
    weight_copy.start()
    columns = jnp.transpose(columns_ref[...].reshape(shares * share, cells)).astype(F32)
    average = jnp.mean(columns, axis=1, keepdims=True)
    series = columns - average
    combined = COEFFS[0] * series
    for copy in copies + [weight_copy]:
        copy.wait()
    for power in range(1, DEGREE + 1):
        projected = lax.dot_general(
            series.astype(BF16), observed_ref[...], (((1,), (1,)), ((), ())), preferred_element_type=F32
        )
        scaled = (projected * weight_ref[...]).astype(BF16)
        series = jnp.dot(scaled, observed_ref[...], preferred_element_type=F32)
        combined = combined + COEFFS[power] * series
    analysed = (average + combined).astype(BF16)
    analysed_ref[...] = jnp.transpose(analysed).reshape(shares, share, cells)


def unpack(members, rows, returned_ref, out_ref):
    for row in range(rows):
        for side in range(2):
            out_ref[pl.ds(side * rows + row, members, stride=2 * rows), :] = returned_ref[2 * row + side].astype(F32)


def shards(state, courant, obs_pert, obs_cell, block_rows, band_list):
    members, rows, lon = state.shape
    bands = lax.axis_size("band")
    shares = lax.axis_size("mem")
    obs_rows, all_members = obs_pert.shape[1:]
    cells = rows * lon // shares
    message = pltpu.VMEM((STEPS, members + EXTRA, lon), BF16)
    towards_a, towards_b, fields = pl.pallas_call(
        functools.partial(pack, members, rows),
        out_shape=(message, message, pltpu.VMEM((rows, members, lon), F32)),
        in_specs=[VMEM] * 3,
        out_specs=(VMEM,) * 3,
        compiler_params=PARAMS,
        name="pack",
    )(state.reshape(members, rows, lon // LANES, LANES).transpose(0, 2, 1, 3).reshape(-1, LANES), courant, obs_cell)
    pairs_a = [(band, band ^ 1) for band in range(bands)]
    pairs_b = [(band, (band + (1 if band % 2 else -1)) % bands) for band in range(bands)]
    from_b = lax.ppermute(towards_b, "band", pairs_b)
    from_a = lax.ppermute(towards_a, "band", pairs_a)
    ring = [
        (band * shares + mem, (band + (-1 if mem % 2 else 1)) % bands * shares + mem)
        for band in range(bands)
        for mem in range(shares)
    ]
    source, _ = lax.optimization_barrier((obs_pert, towards_b))
    fetched = lax.ppermute(source, ("band", "mem"), ring)
    groups, near = pl.pallas_call(
        functools.partial(advect, members, rows),
        out_shape=(
            pltpu.VMEM((shares, members, cells), BF16),
            jax.ShapeDtypeStruct((2, EXTRA, lon), F32),
        ),
        in_specs=[VMEM] * 4,
        out_specs=(VMEM,) * 2,
        scratch_shapes=[
            pltpu.VMEM((rows + 2 * STEPS, members, lon), F32),
            pltpu.VMEM((rows + 2 * STEPS, 4, 8, lon), F32),
        ],
        compiler_params=PARAMS,
        name="advect",
    )(in_vmem(fields), courant, in_vmem(from_a), in_vmem(from_b))
    columns = lax.all_to_all(groups, "mem", split_axis=0, concat_axis=0, tiled=True)
    held, _ = lax.optimization_barrier((fetched, groups))
    swapped = lax.ppermute(held, "mem", [(mem, mem ^ 1) for mem in range(shares)])
    weight = pl.pallas_call(
        functools.partial(localize, rows, lon, 1.0 / (all_members + LIST * obs_rows)),
        out_shape=jax.ShapeDtypeStruct((cells, LIST * obs_rows), F32),
        in_specs=[SMEM, SMEM, VMEM, VMEM],
        out_specs=VMEM,
        compiler_params=PARAMS,
        name="localize",
    )(band_list, block_rows, obs_cell, near)
    analysed = pl.pallas_call(
        transform,
        out_shape=pltpu.VMEM((shares, members, cells), BF16),
        in_specs=[SMEM, VMEM, ANY, ANY, ANY, ANY],
        out_specs=VMEM,
        scratch_shapes=[
            pltpu.VMEM((LIST * obs_rows, all_members), BF16),
            pltpu.VMEM((cells, LIST * obs_rows), F32),
            pltpu.SemaphoreType.DMA((LIST + 1,)),
        ],
        compiler_params=PARAMS,
        name="transform",
    )(band_list, in_vmem(columns), weight, obs_pert, fetched, swapped)
    returned = lax.all_to_all(analysed, "mem", split_axis=0, concat_axis=0, tiled=True)
    out = pl.pallas_call(
        functools.partial(unpack, members, rows),
        out_shape=jax.ShapeDtypeStruct((members * 2 * rows, LANES), F32),
        in_specs=[VMEM],
        out_specs=VMEM,
        compiler_params=pltpu.CompilerParams(vmem_limit_bytes=16 << 20),
        name="unpack",
    )(in_vmem(returned))
    return out.reshape(members, 2, rows, LANES).transpose(0, 2, 1, 3).reshape(members, rows, lon)


def solution(mesh):
    return jax.shard_map(
        shards,
        mesh=mesh,
        in_specs=(
            P("mem", "band", None),
            P(None, "band", None),
            P("band", None, None),
            P("band", None),
            P(),
            P("band", None),
        ),
        out_specs=P("mem", "band", None),
        check_vma=False,
    )
```

time: 184 us -> 92.9 us (0.50)
  starting transfers between devices: 79.8 us -> 36.6 us
  waiting for transfers between devices: 49.1 us -> 22.4 us
  Pallas kernels: 0 us -> 15.8 us
  matrix products: 14.9 us -> 0 us
  local copies, waits for them, and re-layouts: 10.4 us -> 3.1 us
  blocking collectives: 20 us -> 14.5 us
  between operations: 4.35 us -> 0.1 us
  other arithmetic: 4.23 us -> 0 us
    ppermute x16 -> x4, starting transfers between devices: 63.3 us -> 29.3 us  [the longest x1 21.1 us: shards(): fetched = lax.ppermute(source, ('band', 'mem'), ring)]
    ppermute x16 -> x4, waiting for transfers between devices: 33.8 us -> 12.3 us  [the longest x1 9.52 us: shards(): from_b = lax.ppermute(towards_b, 'band', pairs_b)]
    pallas_call x0 -> x5, Pallas kernels: none -> 15.8 us  [the longest x1 7.73 us: shards(): pl.pallas_call(functools.partial(advect, members, rows), out_shape=(pltpu...]
    dot_general x4 -> x0, matrix products: 14.9 us -> none  [transform(): lax.dot_general(observed, scaled, (((0,), (0,)), ((), ())), preferred_ele...]
    all_to_all x1, starting transfers between devices: 16.5 us -> 7.24 us  [shards(): lax.all_to_all(groups, 'mem', split_axis=0, concat_axis=0, tiled=True)]
    slice x19 -> x0, local copies, waits for them, and re-layouts: 6.51 us -> none  [the longest x12 4.2 us: advance(): western = jnp.roll(centre, 1, axis=2)]
    all_to_all x1, blocking collectives: 20 us -> 14.5 us  [shards(): lax.all_to_all(analysed, 'mem', split_axis=0, concat_axis=0, tiled=True)]
    all_to_all x1, waiting for transfers between devices: 15.3 us -> 10.1 us  [shards(): lax.all_to_all(groups, 'mem', split_axis=0, concat_axis=0, tiled=True)]
  transfers between devices with their start and end apart: 17 -> 5, of which waited for: 8 -> 3; matrix products, arithmetic and copies ran while one was open for 7% -> 0% of each run, Pallas kernels for 0% -> 9%
where the time goes in v1:
time: 92.9 us; the launch traced here: 92.4 us
  starting transfers between devices  36.6 us (39%)
  waiting for transfers between devices  22.4 us (24%)
  Pallas kernels  15.8 us (17%)
  blocking collectives  14.5 us (16%)
  local copies, waits for them, and re-layouts  3.1 us (3%)
    ppermute x1, starting transfers between devices, shards(): fetched = lax.ppermute(source, ('band', 'mem'), ring)  21.1 us
    all_to_all x1, blocking collectives, shards(): lax.all_to_all(analysed, 'mem', split_axis=0, concat_axis=0, tiled=True)  14.5 us
    all_to_all x1, waiting for transfers between devices, shards(): lax.all_to_all(groups, 'mem', split_axis=0, concat_axis=0, tiled=True)  10.1 us
    ppermute x1, waiting for transfers between devices, shards(): from_b = lax.ppermute(towards_b, 'band', pairs_b)  9.52 us
    pallas_call x1, Pallas kernels, shards(): pl.pallas_call(functools.partial(advect, members, rows), out_shape=(pltpu...  7.73 us
    all_to_all x1, starting transfers between devices, shards(): lax.all_to_all(groups, 'mem', split_axis=0, concat_axis=0, tiled=True)  7.24 us
    pallas_call x1, Pallas kernels, shards(): pl.pallas_call(transform, out_shape=pltpu.VMEM((shares, members, cells),...  5.95 us
    ppermute x1, starting transfers between devices, shards(): lax.ppermute(held, 'mem', [(mem, mem ^ 1) for mem in range(shares)])  3.9 us
  transfers between devices with their start and end apart: 5, of which 3 were waited for; matrix products, arithmetic and copies ran while one was open for 0% of the time, Pallas kernels for 9%

profile of v1, /device:TPU:1, one launch (start us, length us, event | category | flops | bytes accessed | tf_op | source)
XLA Modules:
  0.0 92.4 jit_solution(246367296505060856)
XLA Ops:
  0.0 0.0 copy-start.1
  0.0 1.0 %copy-done.1 = f32[64,8,256]{2,1,0:T(8,128)S(1)} copy-done((f32[64,8,256]{2,1,0:T(8,128)S(1)}, f32[64,8,256]{2,1,0:T(8,128)}, u32[]{:S(2)}) %copy-start.1) | copy-done | bytes 524312
  1.0 0.0 copy-start.2
  1.0 0.7 copy-done.2
  1.8 0.0 copy-start.3
  1.8 0.7 copy-done.3
  2.4 0.2 pack.1
  2.7 0.0 copy-start
  2.7 21.1 %collective-permute-start.2 = (bf16[1,512,1024]{2,1,0:T(8,128)(2,1)}, bf16[1,512,1024]{2,1,0:T(8,128)(2,1)S(1)}, u32[]{:S(2)}, u32[]{:S(2)}) collective-permute-start(bf16[1,512,1024]{2,1,0:T(8,128)(2,1)} %own_ref.1), channel_id=1, source_target_pairs={{0,16},{1,1009},{2,18},{3,1011},{4,20},{5,1013},{6,22},{7,1015},{8... | collective-permute-start | bytes 3145736 | tf_op jit(solution)/shard_map/ppermute | solution.py:246
  23.8 1.9 %collective-permute-start = (bf16[6,72,256]{2,1,0:T(8,128)(2,1)S(1)}, bf16[6,72,256]{2,1,0:T(8,128)(2,1)S(1)}, u32[]{:S(2)}, u32[]{:S(2)}) collective-permute-start(bf16[6,72,256]{2,1,0:T(8,128)(2,1)S(1)} %get-tuple-element.13), channel_id=1, source_target_pairs={{0,16},{16,0},{32,48},{48,32},{64,80},{80,64},{96,112},{112,96},{1... | collective-permute-start | bytes 663560 | tf_op jit(solution)/shard_map/ppermute | solution.py:239
  25.7 2.4 %collective-permute-start.1 = (bf16[6,72,256]{2,1,0:T(8,128)(2,1)S(1)}, bf16[6,72,256]{2,1,0:T(8,128)(2,1)S(1)}, u32[]{:S(2)}, u32[]{:S(2)}) collective-permute-start(bf16[6,72,256]{2,1,0:T(8,128)(2,1)S(1)} %get-tuple-element.14), channel_id=1, source_target_pairs={{0,1008},{16,32},{32,16},{48,64},{64,48},{80,96},{96,80},{112,128}... | collective-permute-start | bytes 663560 | tf_op jit(solution)/shard_map/ppermute | solution.py:238
  28.2 2.8 %collective-permute-done.from_a_ref = bf16[6,72,256]{2,1,0:T(8,128)(2,1)S(1)} collective-permute-done((bf16[6,72,256]{2,1,0:T(8,128)(2,1)S(1)}, bf16[6,72,256]{2,1,0:T(8,128)(2,1)S(1)}, u32[]{:S(2)}, u32[]{:S(2)}) %collective-permute-start) | collective-permute-done | bytes 221216 | tf_op jit(solution)/shard_map/ppermute | solution.py:239
  31.0 9.5 %collective-permute-done.1.from_b_ref = bf16[6,72,256]{2,1,0:T(8,128)(2,1)S(1)} collective-permute-done((bf16[6,72,256]{2,1,0:T(8,128)(2,1)S(1)}, bf16[6,72,256]{2,1,0:T(8,128)(2,1)S(1)}, u32[]{:S(2)}, u32[]{:S(2)}) %collective-permute-start.1) | collective-permute-done | bytes 221216 | tf_op jit(solution)/shard_map/ppermute | solution.py:238
  40.5 7.7 %advect.1 = (bf16[16,64,128]{2,1,0:T(8,128)(2,1)}, f32[2,8,256]{2,1,0:T(8,128)S(1)}) custom-call(f32[8,64,256]{2,1,0:T(8,128)S(1)} %get-tuple-element.12.fields_ref, f32[2,8,256]{2,1,0:T(8,128)S(1)} %copy-done.2, bf16[6,72,256]{2,1,0:T(8,128)(2,1)S(1)} %collective-permute-done.from_a_ref, bf16[6,72,256]{2,1,0:T(8,128)(2,1)S(1)} %collective-permute-done.1.from_b_ref), custom_call_target="tpu_custom_call" | custom-call | tf_op jit(solution)/shard_map/advect/pallas_call | solution.py:247
  48.2 0.0 collective-permute-done.2.fetched_ref
  48.2 3.9 %collective-permute-start.3 = (bf16[1,512,1024]{2,1,0:T(8,128)(2,1)S(1)}, bf16[1,512,1024]{2,1,0:T(8,128)(2,1)}, u32[]{:S(2)}, u32[]{:S(2)}) collective-permute-start(bf16[1,512,1024]{2,1,0:T(8,128)(2,1)S(1)} %collective-permute-done.2.fetched_ref), channel_id=1, source_target_pairs={{0,1},{1,0},{2,3},{3,2},{4,5},{5,4},{6,7},{7,6},{8,9},{9,8},{10,11... | collective-permute-start | bytes 3145736 | tf_op jit(solution)/shard_map/ppermute | solution.py:264
  52.1 0.0 copy-start.4
  52.1 7.2 %all-to-all-start = ((bf16[16,64,128]{2,1,0:T(8,128)(2,1)}), bf16[16,64,128]{2,1,0:T(8,128)(2,1)S(1)}, u32[]{:S(2)}, u32[]{:S(2)}) async-start(bf16[16,64,128]{2,1,0:T(8,128)(2,1)} %get-tuple-element.15), calls=%async_computation | async-start | bytes 524288 | tf_op jit(solution)/shard_map/all_to_all | solution.py:262
  59.4 0.0 copy-start.5
  59.4 0.0 copy-start.6
  59.4 0.0 copy-done.4
  59.4 0.6 copy-done.5
  60.0 0.0 copy-done.6
  60.0 0.8 localize.1.weight_hbm
  60.8 10.1 %all-to-all-done.columns_ref = bf16[16,64,128]{2,1,0:T(8,128)(2,1)S(1)} async-done(((bf16[16,64,128]{2,1,0:T(8,128)(2,1)}), bf16[16,64,128]{2,1,0:T(8,128)(2,1)S(1)}, u32[]{:S(2)}, u32[]{:S(2)}) %all-to-all-start) | async-done | bytes 262176 | tf_op jit(solution)/shard_map/all_to_all | solution.py:262
  71.0 0.0 collective-permute-done.3.swapped_ref
  71.0 0.0 copy-done
  71.0 5.9 %transform.1 = bf16[16,64,128]{2,1,0:T(8,128)(2,1)S(1)} custom-call(s32[1,2]{1,0:T(1,128)S(1)} %copy-done.5, bf16[16,64,128]{2,1,0:T(8,128)(2,1)S(1)} %all-to-all-done.columns_ref, f32[128,1024]{1,0:T(8,128)S(1)} %localize.1.weight_hbm, bf16[1,512,1024]{2,1,0:T(8,128)(2,1)S(1)} %copy-done, bf16[1,512,1024]{2,1,0:T(8,128)(2,1)S(1)} %collective-permute-done.2.fetched_ref, ...), custom_call_target="tpu_custom_call" | custom-call | tf_op jit(solution)/shard_map/transform/pallas_call | solution.py:273
  76.9 14.5 %all_to_all.10.returned_ref = bf16[16,64,128]{2,1,0:T(8,128)(2,1)S(1)} all-to-all(bf16[16,64,128]{2,1,0:T(8,128)(2,1)S(1)} %transform.1), channel_id=1, replica_groups=mesh['band'=64,'mem'=16] {'mem'}, dimensions={0} | all-to-all | bytes 524288 | tf_op jit(solution)/shard_map/all_to_all | solution.py:286
  91.4 1.0 %unpack.1 = f32[1024,128]{1,0:T(8,128)} custom-call(bf16[16,64,128]{2,1,0:T(8,128)(2,1)S(1)} %all_to_all.10.returned_ref), custom_call_target="tpu_custom_call" | custom-call | tf_op jit(solution)/shard_map/unpack/pallas_call | solution.py:287
Async XLA Ops:
  0.0 1.0 %copy-start.1 = (f32[64,8,256]{2,1,0:T(8,128)S(1)}, f32[64,8,256]{2,1,0:T(8,128)}, u32[]{:S(2)}) copy-start(f32[64,8,256]{2,1,0:T(8,128)} %param.6) | copy-start | bytes 1572868
  1.0 0.7 copy-start.2
  1.8 0.7 copy-start.3
  2.7 68.3 %copy-start = (bf16[1,512,1024]{2,1,0:T(8,128)(2,1)S(1)}, bf16[1,512,1024]{2,1,0:T(8,128)(2,1)}, u32[]{:S(2)}) copy-start(bf16[1,512,1024]{2,1,0:T(8,128)(2,1)} %own_ref.1) | copy-start | bytes 3145732
  2.7 45.5 %collective-permute-start.2 = (bf16[1,512,1024]{2,1,0:T(8,128)(2,1)}, bf16[1,512,1024]{2,1,0:T(8,128)(2,1)S(1)}, u32[]{:S(2)}, u32[]{:S(2)}) collective-permute-start(bf16[1,512,1024]{2,1,0:T(8,128)(2,1)} %own_ref.1), channel_id=1, source_target_pairs={{0,16},{1,1009},{2,18},{3,1011},{4,20},{5,1013},{6,22},{7,1015},{8... | collective-permute-start | bytes 3145736 | tf_op jit(solution)/shard_map/ppermute | solution.py:246
  23.8 7.2 %collective-permute-start = (bf16[6,72,256]{2,1,0:T(8,128)(2,1)S(1)}, bf16[6,72,256]{2,1,0:T(8,128)(2,1)S(1)}, u32[]{:S(2)}, u32[]{:S(2)}) collective-permute-start(bf16[6,72,256]{2,1,0:T(8,128)(2,1)S(1)} %get-tuple-element.13), channel_id=1, source_target_pairs={{0,16},{16,0},{32,48},{48,32},{64,80},{80,64},{96,112},{112,96},{1... | collective-permute-start | bytes 663560 | tf_op jit(solution)/shard_map/ppermute | solution.py:239
  25.7 14.7 %collective-permute-start.1 = (bf16[6,72,256]{2,1,0:T(8,128)(2,1)S(1)}, bf16[6,72,256]{2,1,0:T(8,128)(2,1)S(1)}, u32[]{:S(2)}, u32[]{:S(2)}) collective-permute-start(bf16[6,72,256]{2,1,0:T(8,128)(2,1)S(1)} %get-tuple-element.14), channel_id=1, source_target_pairs={{0,1008},{16,32},{32,16},{48,64},{64,48},{80,96},{96,80},{112,128}... | collective-permute-start | bytes 663560 | tf_op jit(solution)/shard_map/ppermute | solution.py:238
  48.2 22.7 %collective-permute-start.3 = (bf16[1,512,1024]{2,1,0:T(8,128)(2,1)S(1)}, bf16[1,512,1024]{2,1,0:T(8,128)(2,1)}, u32[]{:S(2)}, u32[]{:S(2)}) collective-permute-start(bf16[1,512,1024]{2,1,0:T(8,128)(2,1)S(1)} %collective-permute-done.2.fetched_ref), channel_id=1, source_target_pairs={{0,1},{1,0},{2,3},{3,2},{4,5},{5,4},{6,7},{7,6},{8,9},{9,8},{10,11... | collective-permute-start | bytes 3145736 | tf_op jit(solution)/shard_map/ppermute | solution.py:264
  52.1 7.3 %copy-start.4 = (s32[1,512]{1,0:T(1,128)S(1)}, s32[1,512]{1,0:T(1,128)}, u32[]{:S(2)}) copy-start(s32[1,512]{1,0:T(1,128)} %cells_ref.3) | copy-start | bytes 6148
  52.1 18.8 %all-to-all-start = ((bf16[16,64,128]{2,1,0:T(8,128)(2,1)}), bf16[16,64,128]{2,1,0:T(8,128)(2,1)S(1)}, u32[]{:S(2)}, u32[]{:S(2)}) async-start(bf16[16,64,128]{2,1,0:T(8,128)(2,1)} %get-tuple-element.15), calls=%async_computation | async-start | bytes 524288 | tf_op jit(solution)/shard_map/all_to_all | solution.py:262
  59.4 0.7 copy-start.5
  59.4 0.7 copy-start.6

commit v2 on v1

v2 whole, which is shorter than its diff:
```python
import functools

import jax
import jax.numpy as jnp
from jax import lax
from jax.experimental import pallas as pl
from jax.experimental.pallas import tpu as pltpu
from jax.sharding import PartitionSpec as P


STEPS = 6
LIST = 2
DEGREE = 4

DIFFUSION = 0.05
COEFFS = (1.0, -0.5, 0.375, -0.3125, 0.2734375)

F32 = jnp.float32
BF16 = jnp.bfloat16
VMEM = pl.BlockSpec(memory_space=pltpu.VMEM)
PARAMS = pltpu.CompilerParams(vmem_limit_bytes=16 << 20)
SMEM = pl.BlockSpec(memory_space=pltpu.SMEM)
ANY = pl.BlockSpec(memory_space=pl.ANY)
HBM = pl.BlockSpec(memory_space=pltpu.HBM)

EXTRA = 8
SEND_SCALE = 4096.0
LANES = 128
GROUP = 32


def in_vmem(x):
    return pltpu.with_memory_space_constraint(x, pltpu.VMEM)


def in_hbm(x):
    return pltpu.with_memory_space_constraint(x, pltpu.HBM)


def pack(
    members, rows, state_hbm, courant_hbm, cells_hbm, southward_ref, northward_ref, fields_ref, winds_ref,
    state_ref, courant_ref, cells_ref, sems,
):
    copies = [
        pltpu.make_async_copy(source, target, sems.at[slot])
        for slot, (source, target) in enumerate(
            ((state_hbm, state_ref), (courant_hbm, courant_ref), (cells_hbm, cells_ref))
        )
    ]
    for copy in copies:
        copy.start()
    for copy in copies[1:]:
        copy.wait()
    lon = fields_ref.shape[2]
    sides = lon // LANES
    place = lax.broadcasted_iota(jnp.int32, (EXTRA, lon), 0)
    cells = cells_ref[...]
    lat = jnp.bitwise_and(lax.shift_right_logical(cells, 8), rows - 1).astype(F32)
    east = jnp.bitwise_and(cells, lon - 1).astype(F32)
    obs = jnp.zeros((EXTRA, lon), F32)
    for slot, values in ((4, lat[:, :lon]), (5, lat[:, lon:]), (6, east[:, :lon]), (7, east[:, lon:])):
        obs = jnp.where(place == slot, values, obs)
    for message_ref, first in ((southward_ref, rows - STEPS), (northward_ref, 0)):
        for step in range(STEPS):
            extra = obs
            for wind in range(2):
                value = courant_ref[wind, first + step : first + step + 1, :]
                high = value.astype(BF16).astype(F32)
                extra = jnp.where(place == wind, high, extra)
                extra = jnp.where(place == wind + 2, value - high, extra)
            message_ref[step, members:, :] = extra.astype(BF16)
    for row in range(rows):
        keep_winds(winds_ref, row, courant_ref[0, row : row + 1, :], courant_ref[1, row : row + 1, :])
    copies[0].wait()
    for row in range(rows):
        for side in range(sides):
            lanes = slice(side * LANES, (side + 1) * LANES)
            values = state_ref[pl.ds(side * rows + row, members, stride=sides * rows), :]
            fields_ref[row, :, lanes] = values
            if row >= rows - STEPS:
                southward_ref[row - rows + STEPS, :members, lanes] = values.astype(BF16)
            if row < STEPS:
                northward_ref[row, :members, lanes] = values.astype(BF16)


def keep_winds(winds_ref, row, value0, value1):
    for wind, value in ((0, value0), (1, value1)):
        half = 0.5 * jnp.broadcast_to(value, winds_ref.shape[2:])
        winds_ref[row, 2 * wind] = half
        winds_ref[row, 2 * wind + 1] = half + DIFFUSION


def open_message(members, message_ref, halo_ref, winds_ref):
    for step in range(STEPS):
        halo_ref[step] = message_ref[step, :members, :].astype(F32)
        extra = message_ref[step, members:, :].astype(F32)
        keep_winds(winds_ref, step, extra[0:1] + extra[2:3], extra[1:2] + extra[3:4])


def minus(left, right):
    return [x - y for x, y in zip(left, right)]


def turned(parts, way, edge, lane):
    mixed = [jnp.where(lane == edge, parts[(side - way) % len(parts)], part) for side, part in enumerate(parts)]
    return [pltpu.roll(part, way % LANES, 1) for part in mixed]


def march(values, first, last, wind, lane):
    fresh = {}
    north = minus(values[first], values[first - 1])
    for row in range(first, last + 1):
        centre = values[row]
        south = minus(values[row + 1], centre)
        west = minus(centre, turned(centre, 1, LANES - 1, lane))
        east = turned(west, -1, 0, lane)
        new = []
        for side, value in enumerate(centre):
            curve = jnp.tanh(value)
            new.append(
                value
                - north[side] * (wind(row, 0, side) * curve + wind(row, 1, side))
                - west[side] * (wind(row, 2, side) * curve + wind(row, 3, side))
                + DIFFUSION * (south[side] + east[side])
            )
        fresh[row] = new
        north = south
    return fresh


def by_group(members, lon, body):
    lane = lax.broadcasted_iota(jnp.int32, (GROUP, LANES), 1)
    sides = [slice(side * LANES, (side + 1) * LANES) for side in range(lon // LANES)]

    def run(index, carry):
        group = pl.ds(pl.multiple_of(index * GROUP, GROUP), GROUP)

        def read(ref, row):
            return [ref[row, group, lanes] for lanes in sides]

        def write(ref, row, parts):
            for lanes, part in zip(sides, parts):
                ref[row, group, lanes] = part

        body(read, write, lane)
        return carry

    lax.fori_loop(0, members // GROUP, run, 0)


def wind_of(winds_ref, halo_winds_ref=None, halo_first=0):
    def wind(row, kind, side):
        lanes = slice(side * LANES, (side + 1) * LANES)
        if 0 <= row < winds_ref.shape[0]:
            value = winds_ref[row, kind, :, lanes]
        else:
            value = halo_winds_ref[row - halo_first, kind, :, lanes]
        return jnp.concatenate([value] * (GROUP // value.shape[0]), axis=0)

    return wind


INNER = ((1, 1), (1, 2), (1, 5), (1, 6), (2, 2), (2, 3), (2, 4), (2, 5), (3, 3), (3, 4))
UPPER = ((4, 2), (4, 3), (5, 1), (5, 2), (6, 0), (6, 1))


def inner(members, rows, fields_ref, winds_ref, inner_ref):
    def body(read, write, lane):
        values = {row: read(fields_ref, row) for row in range(rows)}
        for step in range(1, rows // 2):
            values = march(values, step, rows - 1 - step, wind_of(winds_ref), lane)
            for slot, (at, row) in enumerate(INNER):
                if at == step:
                    write(inner_ref, slot, values[row])

    by_group(members, fields_ref.shape[2], body)


def upper(members, rows, fields_ref, winds_ref, inner_ref, message_ref, upper_ref, halo_ref, halo_winds_ref):
    open_message(members, message_ref, halo_ref, halo_winds_ref)
    wind = wind_of(winds_ref, halo_winds_ref, -STEPS)

    def body(read, write, lane):
        values = {row - STEPS: read(halo_ref, row) for row in range(STEPS)}
        values.update({row: read(fields_ref, row) for row in range(2)})
        for step in range(1, STEPS + 1):
            values = march(values, step - STEPS, min(step - 1, rows - 1 - step), wind, lane)
            for row in (step, step + 1):
                if (step, row) in INNER:
                    values[row] = read(inner_ref, INNER.index((step, row)))
            for slot, (at, row) in enumerate(UPPER):
                if at == step:
                    write(upper_ref, slot, values[row])

    by_group(members, fields_ref.shape[2], body)


def lower(
    members, rows, fields_ref, winds_ref, inner_ref, upper_ref, above_ref, message_ref, groups_ref, near_ref,
    halo_ref, halo_winds_ref,
):
    near_ref[0] = above_ref[0, members:, :].astype(F32)
    near_ref[1] = message_ref[0, members:, :].astype(F32)
    open_message(members, message_ref, halo_ref, halo_winds_ref)
    wind = wind_of(winds_ref, halo_winds_ref, rows)
    sides = fields_ref.shape[2] // LANES

    def body(read, write, lane):
        values = {rows + row: read(halo_ref, row) for row in range(STEPS)}
        values.update({row: read(fields_ref, row) for row in (rows - 2, rows - 1)})
        for step in range(1, STEPS + 1):
            values = march(values, rows - step, rows + STEPS - 1 - step, wind, lane)
            for row in (rows - 2 - step, rows - 1 - step):
                if (step, row) in INNER:
                    values[row] = read(inner_ref, INNER.index((step, row)))
                elif (step, row) in UPPER:
                    values[row] = read(upper_ref, UPPER.index((step, row)))
        for row in range(rows):
            for side, part in enumerate(values[row]):
                write(groups_ref, sides * row + side, [part * SEND_SCALE])

    by_group(members, fields_ref.shape[2], body)


def place_of(listed_ref, position):
    band, bands = lax.axis_index("band"), lax.axis_size("band")
    return lax.rem(listed_ref[0, position] - band + 1 + bands, bands)


def localize(rows, lon, gscale, listed_ref, counts_ref, cells_ref, near_ref, weight_ref):
    mem = lax.axis_index("mem")
    group_cells, obs_total = weight_ref.shape
    obs_rows = obs_total // LIST
    cells = cells_ref[...]
    own_lat = jnp.bitwise_and(lax.shift_right_logical(cells, 8), rows - 1).astype(F32)
    own_lon = jnp.bitwise_and(cells, lon - 1).astype(F32)

    def pair(side, slot):
        return jnp.concatenate([near_ref[side, slot : slot + 1, :], near_ref[side, slot + 1 : slot + 2, :]], axis=1)

    halves = lon // group_cells
    cell_row = (mem // halves).astype(F32)
    cell_lon = (
        lax.broadcasted_iota(jnp.int32, (group_cells, obs_rows), 0) + lax.rem(mem, halves) * group_cells
    ).astype(F32)
    lane = lax.broadcasted_iota(jnp.int32, (group_cells, obs_rows), 1)
    for position in range(LIST):
        place = place_of(listed_ref, position)
        lat = jnp.where(place == 0, pair(0, 4), jnp.where(place == 1, own_lat, pair(1, 4)))
        east = jnp.where(place == 0, pair(0, 6), jnp.where(place == 1, own_lon, pair(1, 6)))
        lat_gap = jnp.abs(lat + (place - 1).astype(F32) * rows - cell_row) * (1.0 / rows)
        lon_gap = jnp.abs(jnp.broadcast_to(east, cell_lon.shape) - cell_lon)
        lon_gap = jnp.minimum(lon_gap, lon - lon_gap) * (4.0 / lon)
        decay = jnp.exp(-0.5 * (jnp.broadcast_to(lat_gap * lat_gap, lon_gap.shape) + lon_gap * lon_gap)) * gscale
        live = lane < counts_ref[listed_ref[0, position]]
        weight_ref[:, position * obs_rows : (position + 1) * obs_rows] = jnp.where(live, decay, 0.0)


def transform(
    listed_ref, columns_ref, weight_hbm, own_ref, fetched_ref, swapped_ref, analysed_ref, observed_ref, weight_ref, sems
):
    shares, share, cells = columns_ref.shape
    obs_rows = own_ref.shape[1]
    first_core = lax.rem(lax.axis_index("mem"), 2) == 0
    copies = []
    for position in range(LIST):
        target = observed_ref.at[pl.ds(position * obs_rows, obs_rows), :]
        place = place_of(listed_ref, position)
        near = place != 1
        fetched = jnp.logical_and(near, (place == 0) == first_core)
        swapped = jnp.logical_and(near, (place == 0) != first_core)
        for chosen, source in ((place == 1, own_ref), (fetched, fetched_ref), (swapped, swapped_ref)):
            copy = pltpu.make_async_copy(source.at[0], target, sems.at[position])
            pl.when(chosen)(copy.start)
        copies.append(copy)
    weight_copy = pltpu.make_async_copy(weight_hbm, weight_ref, sems.at[LIST])
    weight_copy.start()
    columns = jnp.transpose(columns_ref[...].reshape(shares * share, cells)) * (1.0 / SEND_SCALE)
    average = jnp.mean(columns, axis=1, keepdims=True)
    series = columns - average
    combined = COEFFS[0] * series
    for copy in copies + [weight_copy]:
        copy.wait()
    for power in range(1, DEGREE + 1):
        projected = lax.dot_general(
            series.astype(BF16), observed_ref[...], (((1,), (1,)), ((), ())), preferred_element_type=F32
        )
        scaled = (projected * weight_ref[...]).astype(BF16)
        series = jnp.dot(scaled, observed_ref[...], preferred_element_type=F32)
        combined = combined + COEFFS[power] * series
    analysed = (average + combined).astype(BF16)
    analysed_ref[...] = jnp.transpose(analysed).reshape(shares, share, cells)


def unpack(members, rows, returned_ref, out_ref):
    for row in range(rows):
        for side in range(2):
            out_ref[pl.ds(side * rows + row, members, stride=2 * rows), :] = returned_ref[2 * row + side].astype(F32)


def shards(state, courant, obs_pert, obs_cell, block_rows, band_list):
    members, rows, lon = state.shape
    bands = lax.axis_size("band")
    shares = lax.axis_size("mem")
    obs_rows, all_members = obs_pert.shape[1:]
    cells = rows * lon // shares
    message = pltpu.VMEM((STEPS, members + EXTRA, lon), BF16)
    halo_scratch = [pltpu.VMEM((STEPS, members, lon), F32), pltpu.VMEM((STEPS, 4, 8, lon), F32)]
    ring = [
        (band * shares + mem, (band + (-1 if mem % 2 else 1)) % bands * shares + mem)
        for band in range(bands)
        for mem in range(shares)
    ]
    southward, northward, fields, winds = pl.pallas_call(
        functools.partial(pack, members, rows),
        out_shape=(
            message,
            message,
            pltpu.VMEM((rows, members, lon), F32),
            pltpu.VMEM((rows, 4, 8, lon), F32),
        ),
        in_specs=[HBM] * 3,
        out_specs=(VMEM,) * 4,
        scratch_shapes=[
            pltpu.VMEM((members * rows * lon // LANES, LANES), F32),
            pltpu.VMEM(courant.shape, F32),
            pltpu.VMEM(obs_cell.shape, jnp.int32),
            pltpu.SemaphoreType.DMA((3,)),
        ],
        compiler_params=PARAMS,
        name="pack",
    )(
        in_hbm(state.reshape(members, rows, lon // LANES, LANES).transpose(0, 2, 1, 3).reshape(-1, LANES)),
        in_hbm(courant),
        in_hbm(obs_cell),
    )
    above = lax.ppermute(southward, "band", [(band, (band + 1) % bands) for band in range(bands)])
    below = lax.ppermute(northward, "band", [((band + 1) % bands, band) for band in range(bands)])
    fields, winds = in_vmem(fields), in_vmem(winds)
    centre = pl.pallas_call(
        functools.partial(inner, members, rows),
        out_shape=pltpu.VMEM((len(INNER), members, lon), F32),
        in_specs=[VMEM] * 2,
        out_specs=VMEM,
        compiler_params=PARAMS,
        name="inner",
    )(fields, winds)
    centre, above = in_vmem(centre), in_vmem(above)
    north = pl.pallas_call(
        functools.partial(upper, members, rows),
        out_shape=pltpu.VMEM((len(UPPER), members, lon), F32),
        in_specs=[VMEM] * 4,
        out_specs=VMEM,
        scratch_shapes=halo_scratch,
        compiler_params=PARAMS,
        name="upper",
    )(fields, winds, centre, above)
    source, _ = lax.optimization_barrier((obs_pert, north))
    fetched = lax.ppermute(source, ("band", "mem"), ring)
    groups, near = pl.pallas_call(
        functools.partial(lower, members, rows),
        out_shape=(
            pltpu.VMEM((shares, members, cells), F32),
            jax.ShapeDtypeStruct((2, EXTRA, lon), F32),
        ),
        in_specs=[VMEM] * 6,
        out_specs=(VMEM,) * 2,
        scratch_shapes=halo_scratch,
        compiler_params=PARAMS,
        name="lower",
    )(fields, winds, centre, in_vmem(north), above, in_vmem(below))
    columns = lax.all_to_all(groups.astype(jnp.float16), "mem", split_axis=0, concat_axis=0, tiled=True)
    columns = columns.astype(F32)
    held, _ = lax.optimization_barrier((fetched, groups))
    swapped = lax.ppermute(held, "mem", [(mem, mem ^ 1) for mem in range(shares)])
    weight = pl.pallas_call(
        functools.partial(localize, rows, lon, 1.0 / (all_members + LIST * obs_rows)),
        out_shape=jax.ShapeDtypeStruct((cells, LIST * obs_rows), F32),
        in_specs=[SMEM, SMEM, VMEM, VMEM],
        out_specs=VMEM,
        compiler_params=PARAMS,
        name="localize",
    )(band_list, block_rows, obs_cell, near)
    analysed = pl.pallas_call(
        transform,
        out_shape=pltpu.VMEM((shares, members, cells), BF16),
        in_specs=[SMEM, VMEM, ANY, ANY, ANY, ANY],
        out_specs=VMEM,
        scratch_shapes=[
            pltpu.VMEM((LIST * obs_rows, all_members), BF16),
            pltpu.VMEM((cells, LIST * obs_rows), F32),
            pltpu.SemaphoreType.DMA((LIST + 1,)),
        ],
        compiler_params=PARAMS,
        name="transform",
    )(band_list, in_vmem(columns), weight, obs_pert, fetched, swapped)
    returned = lax.all_to_all(analysed, "mem", split_axis=0, concat_axis=0, tiled=True)
    out = pl.pallas_call(
        functools.partial(unpack, members, rows),
        out_shape=jax.ShapeDtypeStruct((members * 2 * rows, LANES), F32),
        in_specs=[VMEM],
        out_specs=VMEM,
        compiler_params=pltpu.CompilerParams(vmem_limit_bytes=16 << 20),
        name="unpack",
    )(in_vmem(returned))
    return out.reshape(members, 2, rows, LANES).transpose(0, 2, 1, 3).reshape(members, rows, lon)


def solution(mesh):
    return jax.shard_map(
        shards,
        mesh=mesh,
        in_specs=(
            P("mem", "band", None),
            P(None, "band", None),
            P("band", None, None),
            P("band", None),
            P(),
            P("band", None),
        ),
        out_specs=P("mem", "band", None),
        check_vma=False,
    )
```

time: 92.9 us -> 97.5 us (1.050)
  waiting for transfers between devices: 22.4 us -> 45.7 us
  starting transfers between devices: 36.6 us -> 19.7 us
  local copies, waits for them, and re-layouts: 3.1 us -> 0.66 us
    ppermute x2, waiting for transfers between devices: 12.3 us -> 35.6 us  [the longest x1 20.3 us: shards(): lax.ppermute(southward, 'band', [(band, (band + 1) % bands) for band in r...]
    ppermute x1, starting transfers between devices: 21.1 us -> 3.08 us  [shards(): fetched = lax.ppermute(source, ('band', 'mem'), ring)]
    ppermute x2, starting transfers between devices: 4.36 us -> 7 us  [the longest x1 4.82 us: shards(): lax.ppermute(southward, 'band', [(band, (band + 1) % bands) for band in r...]
    unnamed x14 -> x8, local copies, waits for them, and re-layouts: 3.1 us -> 0.66 us
    ppermute x1, starting transfers between devices: 3.9 us -> 1.92 us  [shards(): lax.ppermute(held, 'mem', [(mem, mem ^ 1) for mem in range(shares)])]
    pallas_call x1 -> x3, Pallas kernels: 7.73 us -> 6.49 us  [the longest x1 3.33 us: shards(): pl.pallas_call(functools.partial(lower, members, rows), out_shape=(pltpu....]
    pallas_call x1, Pallas kernels: 0.25 us -> 1.27 us  [shards(): pl.pallas_call(functools.partial(pack, members, rows), out_shape=(message...]
  transfers between devices with their start and end apart: 5 -> 5, of which waited for: 3 -> 3; matrix products, arithmetic and copies ran while one was open for 0% -> 1% of each run, Pallas kernels for 9% -> 5%
where the time goes in v2:
time: 97.5 us; the launch traced here: 97.1 us
  waiting for transfers between devices  45.7 us (47%)
  starting transfers between devices  19.7 us (20%)
  Pallas kernels  15.5 us (16%)
  blocking collectives  14.5 us (15%)
    ppermute x1, waiting for transfers between devices, shards(): lax.ppermute(southward, 'band', [(band, (band + 1) % bands) for band in r...  20.3 us
    ppermute x1, waiting for transfers between devices, shards(): lax.ppermute(northward, 'band', [((band + 1) % bands, band) for band in r...  15.3 us
    all_to_all x1, blocking collectives, shards(): lax.all_to_all(analysed, 'mem', split_axis=0, concat_axis=0, tiled=True)  14.5 us
    all_to_all x1, waiting for transfers between devices, shards(): lax.all_to_all(groups.astype(jnp.float16), 'mem', split_axis=0, concat_ax...  10.1 us
    all_to_all x1, starting transfers between devices, shards(): lax.all_to_all(groups.astype(jnp.float16), 'mem', split_axis=0, concat_ax...  7.74 us
    pallas_call x1, Pallas kernels, shards(): pl.pallas_call(transform, out_shape=pltpu.VMEM((shares, members, cells),...  5.92 us
    ppermute x1, starting transfers between devices, shards(): lax.ppermute(southward, 'band', [(band, (band + 1) % bands) for band in r...  4.82 us
    pallas_call x1, Pallas kernels, shards(): pl.pallas_call(functools.partial(lower, members, rows), out_shape=(pltpu....  3.33 us
  transfers between devices with their start and end apart: 5, of which 3 were waited for; matrix products, arithmetic and copies ran while one was open for 1% of the time, Pallas kernels for 5%

profile of v2, /device:TPU:1, one launch (start us, length us, event | category | flops | bytes accessed | tf_op | source)
XLA Modules:
  0.0 97.1 jit_solution(11924512794263644613)
XLA Ops:
  0.0 1.3 %pack.1 = (bf16[6,72,256]{2,1,0:T(8,128)(2,1)S(1)}, bf16[6,72,256]{2,1,0:T(8,128)(2,1)S(1)}, f32[8,64,256]{2,1,0:T(8,128)S(1)}, f32[8,4,8,256]{3,2,1,0:T(8,128)S(1)}) custom-call(f32[1024,128]{1,0:T(8,128)} %bitcast.10, f32[2,8,256]{2,1,0:T(8,128)} %courant_hbm.1, s32[1,512]{1,0:T(1,128)} %cells_ref.1), custom_call_target="tpu_custom_call" | custom-call | tf_op jit(solution)/shard_map/pack/pallas_call | solution.py:314
  1.3 4.8 %collective-permute-start = (bf16[6,72,256]{2,1,0:T(8,128)(2,1)S(1)}, bf16[6,72,256]{2,1,0:T(8,128)(2,1)S(1)}, u32[]{:S(2)}, u32[]{:S(2)}) collective-permute-start(bf16[6,72,256]{2,1,0:T(8,128)(2,1)S(1)} %get-tuple-element.15), channel_id=1, source_target_pairs={{0,16},{16,32},{32,48},{48,64},{64,80},{80,96},{96,112},{112,128},... | collective-permute-start | bytes 663560 | tf_op jit(solution)/shard_map/ppermute | solution.py:337
  6.1 0.9 inner.1.inner_ref
  7.0 0.0 copy-start
  7.1 20.3 %collective-permute-done.message_ref.above_ref = bf16[6,72,256]{2,1,0:T(8,128)(2,1)S(1)} collective-permute-done((bf16[6,72,256]{2,1,0:T(8,128)(2,1)S(1)}, bf16[6,72,256]{2,1,0:T(8,128)(2,1)S(1)}, u32[]{:S(2)}, u32[]{:S(2)}) %collective-permute-start) | collective-permute-done | bytes 221216 | tf_op jit(solution)/shard_map/ppermute | solution.py:337
  27.4 2.2 %upper.1.upper_ref = f32[6,64,256]{2,1,0:T(8,128)S(1)} custom-call(f32[8,64,256]{2,1,0:T(8,128)S(1)} %get-tuple-element.13.fields_ref, f32[8,4,8,256]{3,2,1,0:T(8,128)S(1)} %get-tuple-element.14.winds_ref, f32[10,64,256]{2,1,0:T(8,128)S(1)} %inner.1.inner_ref, bf16[6,72,256]{2,1,0:T(8,128)(2,1)S(1)} %collective-permute-done.message_ref.above_ref), custom_call_target="tpu_custom_call" | custom-call | tf_op jit(solution)/shard_map/upper/pallas_call | solution.py:349
  29.6 0.0 copy-done
  29.6 3.1 %collective-permute-start.2 = (bf16[1,512,1024]{2,1,0:T(8,128)(2,1)S(1)}, bf16[1,512,1024]{2,1,0:T(8,128)(2,1)S(1)}, u32[]{:S(2)}, u32[]{:S(2)}) collective-permute-start(bf16[1,512,1024]{2,1,0:T(8,128)(2,1)S(1)} %copy-done), channel_id=1, source_target_pairs={{0,16},{1,1009},{2,18},{3,1011},{4,20},{5,1013},{6,22},{7,1015},{8... | collective-permute-start | bytes 3145736 | tf_op jit(solution)/shard_map/ppermute | solution.py:359
  32.7 2.2 %collective-permute-start.1 = (bf16[6,72,256]{2,1,0:T(8,128)(2,1)S(1)}, bf16[6,72,256]{2,1,0:T(8,128)(2,1)S(1)}, u32[]{:S(2)}, u32[]{:S(2)}) collective-permute-start(bf16[6,72,256]{2,1,0:T(8,128)(2,1)S(1)} %get-tuple-element.16), channel_id=1, source_target_pairs={{16,0},{32,16},{48,32},{64,48},{80,64},{96,80},{112,96},{128,112},... | collective-permute-start | bytes 663560 | tf_op jit(solution)/shard_map/ppermute | solution.py:338
  34.9 15.3 %collective-permute-done.1.message_ref = bf16[6,72,256]{2,1,0:T(8,128)(2,1)S(1)} collective-permute-done((bf16[6,72,256]{2,1,0:T(8,128)(2,1)S(1)}, bf16[6,72,256]{2,1,0:T(8,128)(2,1)S(1)}, u32[]{:S(2)}, u32[]{:S(2)}) %collective-permute-start.1) | collective-permute-done | bytes 221216 | tf_op jit(solution)/shard_map/ppermute | solution.py:338
  50.2 3.3 %lower.1 = (f32[16,64,128]{2,1,0:T(8,128)S(1)}, f32[2,8,256]{2,1,0:T(8,128)S(1)}) custom-call(f32[8,64,256]{2,1,0:T(8,128)S(1)} %get-tuple-element.13.fields_ref, f32[8,4,8,256]{3,2,1,0:T(8,128)S(1)} %get-tuple-element.14.winds_ref, f32[10,64,256]{2,1,0:T(8,128)S(1)} %inner.1.inner_ref, f32[6,64,256]{2,1,0:T(8,128)S(1)} %upper.1.upper_ref, ...), custom_call_target="tpu_custom_call" | custom-call | tf_op jit(solution)/shard_map/lower/pallas_call | solution.py:360
  53.5 0.0 collective-permute-done.2.fetched_ref
  53.5 1.9 %collective-permute-start.3 = (bf16[1,512,1024]{2,1,0:T(8,128)(2,1)S(1)}, bf16[1,512,1024]{2,1,0:T(8,128)(2,1)}, u32[]{:S(2)}, u32[]{:S(2)}) collective-permute-start(bf16[1,512,1024]{2,1,0:T(8,128)(2,1)S(1)} %collective-permute-done.2.fetched_ref), channel_id=1, source_target_pairs={{0,1},{1,0},{2,3},{3,2},{4,5},{5,4},{6,7},{7,6},{8,9},{9,8},{10,11... | collective-permute-start | bytes 3145736 | tf_op jit(solution)/shard_map/ppermute | solution.py:375
  55.5 0.8 convert_element_type.6
  56.2 0.0 copy-start.1
  56.2 7.7 %all-to-all-start = ((f16[16,64,128]{2,1,0:T(8,128)(2,1)}), f16[16,64,128]{2,1,0:T(8,128)(2,1)S(1)}, u32[]{:S(2)}, u32[]{:S(2)}) async-start(f16[16,64,128]{2,1,0:T(8,128)(2,1)} %convert_element_type.6), calls=%async_computation | async-start | bytes 524288 | tf_op jit(solution)/shard_map/all_to_all | solution.py:372
  64.0 0.0 copy-start.2
  64.0 0.0 copy-start.3
  64.0 0.0 copy-done.1
  64.0 0.6 copy-done.2
  64.6 0.0 copy-done.3
  64.6 0.8 localize.1.weight_hbm
  65.4 10.1 %all-to-all-done = f16[16,64,128]{2,1,0:T(8,128)(2,1)S(1)} async-done(((f16[16,64,128]{2,1,0:T(8,128)(2,1)}), f16[16,64,128]{2,1,0:T(8,128)(2,1)S(1)}, u32[]{:S(2)}, u32[]{:S(2)}) %all-to-all-start) | async-done | bytes 262176 | tf_op jit(solution)/shard_map/all_to_all | solution.py:372
  75.6 0.0 collective-permute-done.3.swapped_ref
  75.6 5.9 %transform.1 = bf16[16,64,128]{2,1,0:T(8,128)(2,1)S(1)} custom-call(s32[1,2]{1,0:T(1,128)S(1)} %copy-done.2, f32[16,64,128]{2,1,0:T(8,128)S(1)} %convert_element_type.7.columns_ref, f32[128,1024]{1,0:T(8,128)S(1)} %localize.1.weight_hbm, bf16[1,512,1024]{2,1,0:T(8,128)(2,1)S(1)} %copy-done, bf16[1,512,1024]{2,1,0:T(8,128)(2,1)S(1)} %collective-permute-done.2.fetched_ref, ...), custom_call_target="tpu_custom_call" | custom-call | tf_op jit(solution)/shard_map/transform/pallas_call | solution.py:384
  81.5 14.5 %all_to_all.10.returned_ref = bf16[16,64,128]{2,1,0:T(8,128)(2,1)S(1)} all-to-all(bf16[16,64,128]{2,1,0:T(8,128)(2,1)S(1)} %transform.1), channel_id=1, replica_groups=mesh['band'=64,'mem'=16] {'mem'}, dimensions={0} | all-to-all | bytes 524288 | tf_op jit(solution)/shard_map/all_to_all | solution.py:397
  96.0 1.0 %unpack.1 = f32[1024,128]{1,0:T(8,128)} custom-call(bf16[16,64,128]{2,1,0:T(8,128)(2,1)S(1)} %all_to_all.10.returned_ref), custom_call_target="tpu_custom_call" | custom-call | tf_op jit(solution)/shard_map/unpack/pallas_call | solution.py:398
  (1 shorter events, 0.0 us)
Async XLA Ops:
  1.3 26.1 %collective-permute-start = (bf16[6,72,256]{2,1,0:T(8,128)(2,1)S(1)}, bf16[6,72,256]{2,1,0:T(8,128)(2,1)S(1)}, u32[]{:S(2)}, u32[]{:S(2)}) collective-permute-start(bf16[6,72,256]{2,1,0:T(8,128)(2,1)S(1)} %get-tuple-element.15), channel_id=1, source_target_pairs={{0,16},{16,32},{32,48},{48,64},{64,80},{80,96},{96,112},{112,128},... | collective-permute-start | bytes 663560 | tf_op jit(solution)/shard_map/ppermute | solution.py:337
  7.0 22.6 %copy-start = (bf16[1,512,1024]{2,1,0:T(8,128)(2,1)S(1)}, bf16[1,512,1024]{2,1,0:T(8,128)(2,1)}, u32[]{:S(2)}) copy-start(bf16[1,512,1024]{2,1,0:T(8,128)(2,1)} %own_ref.1) | copy-start | bytes 3145732
  29.6 23.9 %collective-permute-start.2 = (bf16[1,512,1024]{2,1,0:T(8,128)(2,1)S(1)}, bf16[1,512,1024]{2,1,0:T(8,128)(2,1)S(1)}, u32[]{:S(2)}, u32[]{:S(2)}) collective-permute-start(bf16[1,512,1024]{2,1,0:T(8,128)(2,1)S(1)} %copy-done), channel_id=1, source_target_pairs={{0,16},{1,1009},{2,18},{3,1011},{4,20},{5,1013},{6,22},{7,1015},{8... | collective-permute-start | bytes 3145736 | tf_op jit(solution)/shard_map/ppermute | solution.py:359
  32.7 17.5 %collective-permute-start.1 = (bf16[6,72,256]{2,1,0:T(8,128)(2,1)S(1)}, bf16[6,72,256]{2,1,0:T(8,128)(2,1)S(1)}, u32[]{:S(2)}, u32[]{:S(2)}) collective-permute-start(bf16[6,72,256]{2,1,0:T(8,128)(2,1)S(1)} %get-tuple-element.16), channel_id=1, source_target_pairs={{16,0},{32,16},{48,32},{64,48},{80,64},{96,80},{112,96},{128,112},... | collective-permute-start | bytes 663560 | tf_op jit(solution)/shard_map/ppermute | solution.py:338
  53.5 22.1 %collective-permute-start.3 = (bf16[1,512,1024]{2,1,0:T(8,128)(2,1)S(1)}, bf16[1,512,1024]{2,1,0:T(8,128)(2,1)}, u32[]{:S(2)}, u32[]{:S(2)}) collective-permute-start(bf16[1,512,1024]{2,1,0:T(8,128)(2,1)S(1)} %collective-permute-done.2.fetched_ref), channel_id=1, source_target_pairs={{0,1},{1,0},{2,3},{3,2},{4,5},{5,4},{6,7},{7,6},{8,9},{9,8},{10,11... | collective-permute-start | bytes 3145736 | tf_op jit(solution)/shard_map/ppermute | solution.py:375
  56.2 7.8 %copy-start.1 = (s32[1,512]{1,0:T(1,128)S(1)}, s32[1,512]{1,0:T(1,128)}, u32[]{:S(2)}) copy-start(s32[1,512]{1,0:T(1,128)} %cells_ref.1) | copy-start | bytes 6148
  56.2 19.3 %all-to-all-start = ((f16[16,64,128]{2,1,0:T(8,128)(2,1)}), f16[16,64,128]{2,1,0:T(8,128)(2,1)S(1)}, u32[]{:S(2)}, u32[]{:S(2)}) async-start(f16[16,64,128]{2,1,0:T(8,128)(2,1)} %convert_element_type.6), calls=%async_computation | async-start | bytes 524288 | tf_op jit(solution)/shard_map/all_to_all | solution.py:372
  64.0 0.7 copy-start.2
  64.0 0.7 copy-start.3

commit v3 on v2

--- a/solution.py
+++ b/solution.py
@@ -26,7 +26,6 @@
 EXTRA = 8
 SEND_SCALE = 4096.0
 LANES = 128
-GROUP = 32
 
 
 def in_vmem(x):
@@ -128,12 +127,12 @@
     return fresh
 
 
-def by_group(members, lon, body):
-    lane = lax.broadcasted_iota(jnp.int32, (GROUP, LANES), 1)
+def by_group(members, lon, body, size=32, unroll=1):
+    lane = lax.broadcasted_iota(jnp.int32, (size, LANES), 1)
     sides = [slice(side * LANES, (side + 1) * LANES) for side in range(lon // LANES)]
 
     def run(index, carry):
-        group = pl.ds(pl.multiple_of(index * GROUP, GROUP), GROUP)
+        group = pl.ds(pl.multiple_of(index * size, size), size)
 
         def read(ref, row):
             return [ref[row, group, lanes] for lanes in sides]
@@ -145,17 +144,17 @@
         body(read, write, lane)
         return carry
 
-    lax.fori_loop(0, members // GROUP, run, 0)
-
-
-def wind_of(winds_ref, halo_winds_ref=None, halo_first=0):
+    lax.fori_loop(0, members // size, run, 0, unroll=unroll)
+
+
+def wind_of(size, winds_ref, halo_winds_ref=None, halo_first=0):
     def wind(row, kind, side):
         lanes = slice(side * LANES, (side + 1) * LANES)
         if 0 <= row < winds_ref.shape[0]:
             value = winds_ref[row, kind, :, lanes]
         else:
             value = halo_winds_ref[row - halo_first, kind, :, lanes]
-        return jnp.concatenate([value] * (GROUP // value.shape[0]), axis=0)
+        return jnp.concatenate([value] * (size // value.shape[0]), axis=0)
 
     return wind
 
@@ -168,7 +167,7 @@
     def body(read, write, lane):
         values = {row: read(fields_ref, row) for row in range(rows)}
         for step in range(1, rows // 2):
-            values = march(values, step, rows - 1 - step, wind_of(winds_ref), lane)
+            values = march(values, step, rows - 1 - step, wind_of(32, winds_ref), lane)
             for slot, (at, row) in enumerate(INNER):
                 if at == step:
                     write(inner_ref, slot, values[row])
@@ -178,7 +177,7 @@
 
 def upper(members, rows, fields_ref, winds_ref, inner_ref, message_ref, upper_ref, halo_ref, halo_winds_ref):
     open_message(members, message_ref, halo_ref, halo_winds_ref)
-    wind = wind_of(winds_ref, halo_winds_ref, -STEPS)
+    wind = wind_of(32, winds_ref, halo_winds_ref, -STEPS)
 
     def body(read, write, lane):
         values = {row - STEPS: read(halo_ref, row) for row in range(STEPS)}
@@ -202,7 +201,7 @@
     near_ref[0] = above_ref[0, members:, :].astype(F32)
     near_ref[1] = message_ref[0, members:, :].astype(F32)
     open_message(members, message_ref, halo_ref, halo_winds_ref)
-    wind = wind_of(winds_ref, halo_winds_ref, rows)
+    wind = wind_of(16, winds_ref, halo_winds_ref, rows)
     sides = fields_ref.shape[2] // LANES
 
     def body(read, write, lane):
@@ -219,7 +218,7 @@
             for side, part in enumerate(values[row]):
                 write(groups_ref, sides * row + side, [part * SEND_SCALE])
 
-    by_group(members, fields_ref.shape[2], body)
+    by_group(members, fields_ref.shape[2], body, 16, 2)
 
 
 def place_of(listed_ref, position):
@@ -257,7 +256,8 @@
 
 
 def transform(
-    listed_ref, columns_ref, weight_hbm, own_ref, fetched_ref, swapped_ref, analysed_ref, observed_ref, weight_ref, sems
+    listed_ref, columns_ref, weight_hbm, own_ref, fetched_ref, swapped_ref, analysed_ref,
+    observed_ref, weight_ref, series_ref, scaled_ref, combined_ref, sems,
 ):
     shares, share, cells = columns_ref.shape
     obs_rows = own_ref.shape[1]
@@ -273,23 +273,34 @@
             copy = pltpu.make_async_copy(source.at[0], target, sems.at[position])
             pl.when(chosen)(copy.start)
         copies.append(copy)
-    weight_copy = pltpu.make_async_copy(weight_hbm, weight_ref, sems.at[LIST])
-    weight_copy.start()
+        if position == 0:
+            weight_copy = pltpu.make_async_copy(weight_hbm, weight_ref, sems.at[LIST])
+            weight_copy.start()
     columns = jnp.transpose(columns_ref[...].reshape(shares * share, cells)) * (1.0 / SEND_SCALE)
     average = jnp.mean(columns, axis=1, keepdims=True)
-    series = columns - average
-    combined = COEFFS[0] * series
-    for copy in copies + [weight_copy]:
-        copy.wait()
+    series_ref[...] = (columns - average).astype(BF16)
+    combined_ref[...] = columns
+    blocks = [slice(position * obs_rows, (position + 1) * obs_rows) for position in range(LIST)]
+    halves = [slice(half * obs_rows, (half + 1) * obs_rows) for half in range(shares * share // obs_rows)]
     for power in range(1, DEGREE + 1):
-        projected = lax.dot_general(
-            series.astype(BF16), observed_ref[...], (((1,), (1,)), ((), ())), preferred_element_type=F32
-        )
-        scaled = (projected * weight_ref[...]).astype(BF16)
-        series = jnp.dot(scaled, observed_ref[...], preferred_element_type=F32)
-        combined = combined + COEFFS[power] * series
-    analysed = (average + combined).astype(BF16)
-    analysed_ref[...] = jnp.transpose(analysed).reshape(shares, share, cells)
+        for position, block in enumerate(blocks):
+            if power == 1:
+                copies[position].wait()
+            projected = lax.dot_general(
+                series_ref[...], observed_ref[block, :], (((1,), (1,)), ((), ())), preferred_element_type=F32
+            )
+            if power == 1 and position == 0:
+                weight_copy.wait()
+            scaled_ref[:, block] = (projected * weight_ref[:, block]).astype(BF16)
+        for half in halves:
+            series = jnp.dot(scaled_ref[...], observed_ref[:, half], preferred_element_type=F32)
+            combined = combined_ref[:, half] + COEFFS[power] * series
+            if power < DEGREE:
+                series_ref[:, half] = series.astype(BF16)
+                combined_ref[:, half] = combined
+            else:
+                first, last = half.start // share, half.stop // share
+                analysed_ref[first:last] = jnp.transpose(combined.astype(BF16)).reshape(last - first, share, cells)
 
 
 def unpack(members, rows, returned_ref, out_ref):
@@ -345,6 +356,8 @@
         compiler_params=PARAMS,
         name="inner",
     )(fields, winds)
+    source, _ = lax.optimization_barrier((obs_pert, centre))
+    fetched = lax.ppermute(source, ("band", "mem"), ring)
     centre, above = in_vmem(centre), in_vmem(above)
     north = pl.pallas_call(
         functools.partial(upper, members, rows),
@@ -355,8 +368,6 @@
         compiler_params=PARAMS,
         name="upper",
     )(fields, winds, centre, above)
-    source, _ = lax.optimization_barrier((obs_pert, north))
-    fetched = lax.ppermute(source, ("band", "mem"), ring)
     groups, near = pl.pallas_call(
         functools.partial(lower, members, rows),
         out_shape=(
@@ -389,6 +400,9 @@
         scratch_shapes=[
             pltpu.VMEM((LIST * obs_rows, all_members), BF16),
             pltpu.VMEM((cells, LIST * obs_rows), F32),
+            pltpu.VMEM((cells, all_members), BF16),
+            pltpu.VMEM((cells, LIST * obs_rows), BF16),
+            pltpu.VMEM((cells, all_members), F32),
             pltpu.SemaphoreType.DMA((LIST + 1,)),
         ],
         compiler_params=PARAMS,

time: 97.5 us -> 90.2 us (0.925)
  waiting for transfers between devices: 45.7 us -> 15.7 us
  starting transfers between devices: 19.7 us -> 43.1 us
    ppermute x1, starting transfers between devices: 3.08 us -> 21 us  [shards(): fetched = lax.ppermute(source, ('band', 'mem'), ring)]
    ppermute x1, waiting for transfers between devices: 20.3 us -> 4.04 us  [shards(): lax.ppermute(southward, 'band', [(band, (band + 1) % bands) for band in r...]
    ppermute x1, waiting for transfers between devices: 15.3 us -> 1.57 us  [shards(): lax.ppermute(northward, 'band', [((band + 1) % bands, band) for band in r...]
    ppermute x1, starting transfers between devices: 2.18 us -> 6.68 us  [shards(): lax.ppermute(northward, 'band', [((band + 1) % bands, band) for band in r...]
    ppermute x1, starting transfers between devices: 1.92 us -> 6.15 us  [shards(): lax.ppermute(held, 'mem', [(mem, mem ^ 1) for mem in range(shares)])]
    ppermute x1, starting transfers between devices: 4.82 us -> 1.92 us  [shards(): lax.ppermute(southward, 'band', [(band, (band + 1) % bands) for band in r...]
  transfers between devices with their start and end apart: 5 -> 5, of which waited for: 3 -> 3; matrix products, arithmetic and copies ran while one was open for 1% -> 1% of each run, Pallas kernels for 5% -> 6%
where the time goes in v3:
time: 90.2 us; the launch traced here: 89.8 us
  starting transfers between devices  43.1 us (48%)
  waiting for transfers between devices  15.7 us (17%)
  Pallas kernels  15.3 us (17%)
  blocking collectives  14.1 us (16%)
    ppermute x1, starting transfers between devices, shards(): fetched = lax.ppermute(source, ('band', 'mem'), ring)  21 us
    all_to_all x1, blocking collectives, shards(): lax.all_to_all(analysed, 'mem', split_axis=0, concat_axis=0, tiled=True)  14.1 us
    all_to_all x1, waiting for transfers between devices, shards(): lax.all_to_all(groups.astype(jnp.float16), 'mem', split_axis=0, concat_ax...  10.1 us
    all_to_all x1, starting transfers between devices, shards(): lax.all_to_all(groups.astype(jnp.float16), 'mem', split_axis=0, concat_ax...  7.36 us
    ppermute x1, starting transfers between devices, shards(): lax.ppermute(northward, 'band', [((band + 1) % bands, band) for band in r...  6.68 us
    ppermute x1, starting transfers between devices, shards(): lax.ppermute(held, 'mem', [(mem, mem ^ 1) for mem in range(shares)])  6.15 us
    pallas_call x1, Pallas kernels, shards(): pl.pallas_call(transform, out_shape=pltpu.VMEM((shares, members, cells),...  6.12 us
    ppermute x1, waiting for transfers between devices, shards(): lax.ppermute(southward, 'band', [(band, (band + 1) % bands) for band in r...  4.04 us
  transfers between devices with their start and end apart: 5, of which 3 were waited for; matrix products, arithmetic and copies ran while one was open for 1% of the time, Pallas kernels for 6%

profile of v3, /device:TPU:1, one launch (start us, length us, event | category | flops | bytes accessed | tf_op | source)
XLA Modules:
  0.0 89.8 jit_solution(2943833569988435278)
XLA Ops:
  0.0 0.0 copy-start
  0.0 1.4 %pack.1 = (bf16[6,72,256]{2,1,0:T(8,128)(2,1)S(1)}, bf16[6,72,256]{2,1,0:T(8,128)(2,1)S(1)}, f32[8,64,256]{2,1,0:T(8,128)S(1)}, f32[8,4,8,256]{3,2,1,0:T(8,128)S(1)}) custom-call(f32[1024,128]{1,0:T(8,128)} %bitcast.10, f32[2,8,256]{2,1,0:T(8,128)} %courant_hbm.1, s32[1,512]{1,0:T(1,128)} %cells_ref.1), custom_call_target="tpu_custom_call" | custom-call | tf_op jit(solution)/shard_map/pack/pallas_call | solution.py:325
  1.4 0.9 %inner.1.inner_ref = f32[10,64,256]{2,1,0:T(8,128)S(1)} custom-call(f32[8,64,256]{2,1,0:T(8,128)S(1)} %get-tuple-element.13.fields_ref, f32[8,4,8,256]{3,2,1,0:T(8,128)S(1)} %get-tuple-element.14.winds_ref), custom_call_target="tpu_custom_call" | custom-call | tf_op jit(solution)/shard_map/inner/pallas_call | solution.py:351
  2.3 0.0 copy-done
  2.3 21.0 %collective-permute-start.2 = (bf16[1,512,1024]{2,1,0:T(8,128)(2,1)S(1)}, bf16[1,512,1024]{2,1,0:T(8,128)(2,1)S(1)}, u32[]{:S(2)}, u32[]{:S(2)}) collective-permute-start(bf16[1,512,1024]{2,1,0:T(8,128)(2,1)S(1)} %copy-done), channel_id=1, source_target_pairs={{0,16},{1,1009},{2,18},{3,1011},{4,20},{5,1013},{6,22},{7,1015},{8... | collective-permute-start | bytes 3145736 | tf_op jit(solution)/shard_map/ppermute | solution.py:360
  23.3 1.9 %collective-permute-start = (bf16[6,72,256]{2,1,0:T(8,128)(2,1)S(1)}, bf16[6,72,256]{2,1,0:T(8,128)(2,1)S(1)}, u32[]{:S(2)}, u32[]{:S(2)}) collective-permute-start(bf16[6,72,256]{2,1,0:T(8,128)(2,1)S(1)} %get-tuple-element.15), channel_id=1, source_target_pairs={{0,16},{16,32},{32,48},{48,64},{64,80},{80,96},{96,112},{112,128},... | collective-permute-start | bytes 663560 | tf_op jit(solution)/shard_map/ppermute | solution.py:348
  25.2 6.7 %collective-permute-start.1 = (bf16[6,72,256]{2,1,0:T(8,128)(2,1)S(1)}, bf16[6,72,256]{2,1,0:T(8,128)(2,1)S(1)}, u32[]{:S(2)}, u32[]{:S(2)}) collective-permute-start(bf16[6,72,256]{2,1,0:T(8,128)(2,1)S(1)} %get-tuple-element.16), channel_id=1, source_target_pairs={{16,0},{32,16},{48,32},{64,48},{80,64},{96,80},{112,96},{128,112},... | collective-permute-start | bytes 663560 | tf_op jit(solution)/shard_map/ppermute | solution.py:349
  31.9 4.0 %collective-permute-done.message_ref.above_ref = bf16[6,72,256]{2,1,0:T(8,128)(2,1)S(1)} collective-permute-done((bf16[6,72,256]{2,1,0:T(8,128)(2,1)S(1)}, bf16[6,72,256]{2,1,0:T(8,128)(2,1)S(1)}, u32[]{:S(2)}, u32[]{:S(2)}) %collective-permute-start) | collective-permute-done | bytes 221216 | tf_op jit(solution)/shard_map/ppermute | solution.py:348
  35.9 2.2 %upper.1.upper_ref = f32[6,64,256]{2,1,0:T(8,128)S(1)} custom-call(f32[8,64,256]{2,1,0:T(8,128)S(1)} %get-tuple-element.13.fields_ref, f32[8,4,8,256]{3,2,1,0:T(8,128)S(1)} %get-tuple-element.14.winds_ref, f32[10,64,256]{2,1,0:T(8,128)S(1)} %inner.1.inner_ref, bf16[6,72,256]{2,1,0:T(8,128)(2,1)S(1)} %collective-permute-done.message_ref.above_ref), custom_call_target="tpu_custom_call" | custom-call | tf_op jit(solution)/shard_map/upper/pallas_call | solution.py:362
  38.2 1.6 %collective-permute-done.1.message_ref = bf16[6,72,256]{2,1,0:T(8,128)(2,1)S(1)} collective-permute-done((bf16[6,72,256]{2,1,0:T(8,128)(2,1)S(1)}, bf16[6,72,256]{2,1,0:T(8,128)(2,1)S(1)}, u32[]{:S(2)}, u32[]{:S(2)}) %collective-permute-start.1) | collective-permute-done | bytes 221216 | tf_op jit(solution)/shard_map/ppermute | solution.py:349
  39.7 2.8 %lower.1 = (f32[16,64,128]{2,1,0:T(8,128)S(1)}, f32[2,8,256]{2,1,0:T(8,128)S(1)}) custom-call(f32[8,64,256]{2,1,0:T(8,128)S(1)} %get-tuple-element.13.fields_ref, f32[8,4,8,256]{3,2,1,0:T(8,128)S(1)} %get-tuple-element.14.winds_ref, f32[10,64,256]{2,1,0:T(8,128)S(1)} %inner.1.inner_ref, f32[6,64,256]{2,1,0:T(8,128)S(1)} %upper.1.upper_ref, ...), custom_call_target="tpu_custom_call" | custom-call | tf_op jit(solution)/shard_map/lower/pallas_call | solution.py:371
  42.5 0.0 collective-permute-done.2.fetched_ref
  42.6 6.2 %collective-permute-start.3 = (bf16[1,512,1024]{2,1,0:T(8,128)(2,1)S(1)}, bf16[1,512,1024]{2,1,0:T(8,128)(2,1)}, u32[]{:S(2)}, u32[]{:S(2)}) collective-permute-start(bf16[1,512,1024]{2,1,0:T(8,128)(2,1)S(1)} %collective-permute-done.2.fetched_ref), channel_id=1, source_target_pairs={{0,1},{1,0},{2,3},{3,2},{4,5},{5,4},{6,7},{7,6},{8,9},{9,8},{10,11... | collective-permute-start | bytes 3145736 | tf_op jit(solution)/shard_map/ppermute | solution.py:386
  48.7 0.8 convert_element_type.6
  49.5 0.0 copy-start.1
  49.5 7.4 %all-to-all-start = ((f16[16,64,128]{2,1,0:T(8,128)(2,1)}), f16[16,64,128]{2,1,0:T(8,128)(2,1)S(1)}, u32[]{:S(2)}, u32[]{:S(2)}) async-start(f16[16,64,128]{2,1,0:T(8,128)(2,1)} %convert_element_type.6), calls=%async_computation | async-start | bytes 524288 | tf_op jit(solution)/shard_map/all_to_all | solution.py:383
  56.8 0.0 copy-start.2
  56.8 0.0 copy-start.3
  56.9 0.0 copy-done.1
  56.9 0.6 copy-done.2
  57.5 0.0 copy-done.3
  57.5 0.8 localize.1.weight_hbm
  58.3 10.1 %all-to-all-done = f16[16,64,128]{2,1,0:T(8,128)(2,1)S(1)} async-done(((f16[16,64,128]{2,1,0:T(8,128)(2,1)}), f16[16,64,128]{2,1,0:T(8,128)(2,1)S(1)}, u32[]{:S(2)}, u32[]{:S(2)}) %all-to-all-start) | async-done | bytes 262176 | tf_op jit(solution)/shard_map/all_to_all | solution.py:383
  68.5 0.0 collective-permute-done.3.swapped_ref
  68.5 6.1 %transform.1 = bf16[16,64,128]{2,1,0:T(8,128)(2,1)S(1)} custom-call(s32[1,2]{1,0:T(1,128)S(1)} %copy-done.2, f32[16,64,128]{2,1,0:T(8,128)S(1)} %convert_element_type.7.columns_ref, f32[128,1024]{1,0:T(8,128)S(1)} %localize.1.weight_hbm, bf16[1,512,1024]{2,1,0:T(8,128)(2,1)S(1)} %copy-done, bf16[1,512,1024]{2,1,0:T(8,128)(2,1)S(1)} %collective-permute-done.2.fetched_ref, ...), custom_call_target="tpu_custom_call" | custom-call | tf_op jit(solution)/shard_map/transform/pallas_call | solution.py:395
  74.6 14.1 %all_to_all.10.returned_ref = bf16[16,64,128]{2,1,0:T(8,128)(2,1)S(1)} all-to-all(bf16[16,64,128]{2,1,0:T(8,128)(2,1)S(1)} %transform.1), channel_id=1, replica_groups=mesh['band'=64,'mem'=16] {'mem'}, dimensions={0} | all-to-all | bytes 524288 | tf_op jit(solution)/shard_map/all_to_all | solution.py:411
  88.7 1.0 %unpack.1 = f32[1024,128]{1,0:T(8,128)} custom-call(bf16[16,64,128]{2,1,0:T(8,128)(2,1)S(1)} %all_to_all.10.returned_ref), custom_call_target="tpu_custom_call" | custom-call | tf_op jit(solution)/shard_map/unpack/pallas_call | solution.py:412
  (1 shorter events, 0.0 us)
Async XLA Ops:
  0.0 2.3 %copy-start = (bf16[1,512,1024]{2,1,0:T(8,128)(2,1)S(1)}, bf16[1,512,1024]{2,1,0:T(8,128)(2,1)}, u32[]{:S(2)}) copy-start(bf16[1,512,1024]{2,1,0:T(8,128)(2,1)} %own_ref.1) | copy-start | bytes 3145732
  2.3 40.2 %collective-permute-start.2 = (bf16[1,512,1024]{2,1,0:T(8,128)(2,1)S(1)}, bf16[1,512,1024]{2,1,0:T(8,128)(2,1)S(1)}, u32[]{:S(2)}, u32[]{:S(2)}) collective-permute-start(bf16[1,512,1024]{2,1,0:T(8,128)(2,1)S(1)} %copy-done), channel_id=1, source_target_pairs={{0,16},{1,1009},{2,18},{3,1011},{4,20},{5,1013},{6,22},{7,1015},{8... | collective-permute-start | bytes 3145736 | tf_op jit(solution)/shard_map/ppermute | solution.py:360
  23.3 12.7 %collective-permute-start = (bf16[6,72,256]{2,1,0:T(8,128)(2,1)S(1)}, bf16[6,72,256]{2,1,0:T(8,128)(2,1)S(1)}, u32[]{:S(2)}, u32[]{:S(2)}) collective-permute-start(bf16[6,72,256]{2,1,0:T(8,128)(2,1)S(1)} %get-tuple-element.15), channel_id=1, source_target_pairs={{0,16},{16,32},{32,48},{48,64},{64,80},{80,96},{96,112},{112,128},... | collective-permute-start | bytes 663560 | tf_op jit(solution)/shard_map/ppermute | solution.py:348
  25.2 14.5 %collective-permute-start.1 = (bf16[6,72,256]{2,1,0:T(8,128)(2,1)S(1)}, bf16[6,72,256]{2,1,0:T(8,128)(2,1)S(1)}, u32[]{:S(2)}, u32[]{:S(2)}) collective-permute-start(bf16[6,72,256]{2,1,0:T(8,128)(2,1)S(1)} %get-tuple-element.16), channel_id=1, source_target_pairs={{16,0},{32,16},{48,32},{64,48},{80,64},{96,80},{112,96},{128,112},... | collective-permute-start | bytes 663560 | tf_op jit(solution)/shard_map/ppermute | solution.py:349
  42.6 25.9 %collective-permute-start.3 = (bf16[1,512,1024]{2,1,0:T(8,128)(2,1)S(1)}, bf16[1,512,1024]{2,1,0:T(8,128)(2,1)}, u32[]{:S(2)}, u32[]{:S(2)}) collective-permute-start(bf16[1,512,1024]{2,1,0:T(8,128)(2,1)S(1)} %collective-permute-done.2.fetched_ref), channel_id=1, source_target_pairs={{0,1},{1,0},{2,3},{3,2},{4,5},{5,4},{6,7},{7,6},{8,9},{9,8},{10,11... | collective-permute-start | bytes 3145736 | tf_op jit(solution)/shard_map/ppermute | solution.py:386
  49.5 7.4 %copy-start.1 = (s32[1,512]{1,0:T(1,128)S(1)}, s32[1,512]{1,0:T(1,128)}, u32[]{:S(2)}) copy-start(s32[1,512]{1,0:T(1,128)} %cells_ref.1) | copy-start | bytes 6148
  49.5 18.9 %all-to-all-start = ((f16[16,64,128]{2,1,0:T(8,128)(2,1)}), f16[16,64,128]{2,1,0:T(8,128)(2,1)S(1)}, u32[]{:S(2)}, u32[]{:S(2)}) async-start(f16[16,64,128]{2,1,0:T(8,128)(2,1)} %convert_element_type.6), calls=%async_computation | async-start | bytes 524288 | tf_op jit(solution)/shard_map/all_to_all | solution.py:383
  56.8 0.7 copy-start.2
  56.8 0.7 copy-start.3

commit v4 on v3

--- a/solution.py
+++ b/solution.py
@@ -20,11 +20,11 @@
 VMEM = pl.BlockSpec(memory_space=pltpu.VMEM)
 PARAMS = pltpu.CompilerParams(vmem_limit_bytes=16 << 20)
 SMEM = pl.BlockSpec(memory_space=pltpu.SMEM)
-ANY = pl.BlockSpec(memory_space=pl.ANY)
 HBM = pl.BlockSpec(memory_space=pltpu.HBM)
 
-EXTRA = 8
+EXTRA = 16
 SEND_SCALE = 4096.0
+PIECES = 4
 LANES = 128
 
 
@@ -40,15 +40,18 @@
     members, rows, state_hbm, courant_hbm, cells_hbm, southward_ref, northward_ref, fields_ref, winds_ref,
     state_ref, courant_ref, cells_ref, sems,
 ):
-    copies = [
-        pltpu.make_async_copy(source, target, sems.at[slot])
-        for slot, (source, target) in enumerate(
-            ((state_hbm, state_ref), (courant_hbm, courant_ref), (cells_hbm, cells_ref))
-        )
+    length = state_ref.shape[0] // PIECES
+    small = [
+        pltpu.make_async_copy(courant_hbm, courant_ref, sems.at[PIECES]),
+        pltpu.make_async_copy(cells_hbm, cells_ref, sems.at[PIECES + 1]),
     ]
-    for copy in copies:
+    copies = []
+    for piece in range(PIECES):
+        part = pl.ds(piece * length, length)
+        copies.append(pltpu.make_async_copy(state_hbm.at[part], state_ref.at[part], sems.at[piece]))
+    for copy in small + copies:
         copy.start()
-    for copy in copies[1:]:
+    for copy in small:
         copy.wait()
     lon = fields_ref.shape[2]
     sides = lon // LANES
@@ -57,29 +60,30 @@
     lat = jnp.bitwise_and(lax.shift_right_logical(cells, 8), rows - 1).astype(F32)
     east = jnp.bitwise_and(cells, lon - 1).astype(F32)
     obs = jnp.zeros((EXTRA, lon), F32)
-    for slot, values in ((4, lat[:, :lon]), (5, lat[:, lon:]), (6, east[:, :lon]), (7, east[:, lon:])):
+    for slot, values in enumerate((lat[:, :lon], lat[:, lon:], east[:, :lon], east[:, lon:]), 2 * STEPS):
         obs = jnp.where(place == slot, values, obs)
     for message_ref, first in ((southward_ref, rows - STEPS), (northward_ref, 0)):
+        extra = obs
         for step in range(STEPS):
-            extra = obs
             for wind in range(2):
                 value = courant_ref[wind, first + step : first + step + 1, :]
-                high = value.astype(BF16).astype(F32)
-                extra = jnp.where(place == wind, high, extra)
-                extra = jnp.where(place == wind + 2, value - high, extra)
-            message_ref[step, members:, :] = extra.astype(BF16)
+                extra = jnp.where(place == 2 * step + wind, value, extra)
+        message_ref[STEPS * members :, :] = extra.astype(BF16)
     for row in range(rows):
         keep_winds(winds_ref, row, courant_ref[0, row : row + 1, :], courant_ref[1, row : row + 1, :])
-    copies[0].wait()
-    for row in range(rows):
-        for side in range(sides):
-            lanes = slice(side * LANES, (side + 1) * LANES)
-            values = state_ref[pl.ds(side * rows + row, members, stride=sides * rows), :]
-            fields_ref[row, :, lanes] = values
-            if row >= rows - STEPS:
-                southward_ref[row - rows + STEPS, :members, lanes] = values.astype(BF16)
-            if row < STEPS:
-                northward_ref[row, :members, lanes] = values.astype(BF16)
+    share = members // PIECES
+    for piece in range(PIECES):
+        copies[piece].wait()
+        first = piece * share
+        for row in range(rows):
+            for side in range(sides):
+                lanes = slice(side * LANES, (side + 1) * LANES)
+                values = state_ref[pl.ds((first * sides + side) * rows + row, share, stride=sides * rows), :]
+                fields_ref[row, first : first + share, lanes] = values
+                for message_ref, step in ((southward_ref, row - rows + STEPS), (northward_ref, row)):
+                    if 0 <= step < STEPS:
+                        at = step * members + first
+                        message_ref[at : at + share, lanes] = values.astype(BF16)
 
 
 def keep_winds(winds_ref, row, value0, value1):
@@ -90,10 +94,10 @@
 
 
 def open_message(members, message_ref, halo_ref, winds_ref):
+    extra = message_ref[STEPS * members :, :].astype(F32)
     for step in range(STEPS):
-        halo_ref[step] = message_ref[step, :members, :].astype(F32)
-        extra = message_ref[step, members:, :].astype(F32)
-        keep_winds(winds_ref, step, extra[0:1] + extra[2:3], extra[1:2] + extra[3:4])
+        halo_ref[step] = message_ref[step * members : (step + 1) * members, :].astype(F32)
+        keep_winds(winds_ref, step, extra[2 * step : 2 * step + 1], extra[2 * step + 1 : 2 * step + 2])
 
 
 def minus(left, right):
@@ -198,8 +202,8 @@
     members, rows, fields_ref, winds_ref, inner_ref, upper_ref, above_ref, message_ref, groups_ref, near_ref,
     halo_ref, halo_winds_ref,
 ):
-    near_ref[0] = above_ref[0, members:, :].astype(F32)
-    near_ref[1] = message_ref[0, members:, :].astype(F32)
+    for side, ref in enumerate((above_ref, message_ref)):
+        near_ref[side] = ref[STEPS * members :, :].astype(F32)
     open_message(members, message_ref, halo_ref, halo_winds_ref)
     wind = wind_of(16, winds_ref, halo_winds_ref, rows)
     sides = fields_ref.shape[2] // LANES
@@ -245,8 +249,8 @@
     lane = lax.broadcasted_iota(jnp.int32, (group_cells, obs_rows), 1)
     for position in range(LIST):
         place = place_of(listed_ref, position)
-        lat = jnp.where(place == 0, pair(0, 4), jnp.where(place == 1, own_lat, pair(1, 4)))
-        east = jnp.where(place == 0, pair(0, 6), jnp.where(place == 1, own_lon, pair(1, 6)))
+        lat = jnp.where(place == 0, pair(0, 2 * STEPS), jnp.where(place == 1, own_lat, pair(1, 2 * STEPS)))
+        east = jnp.where(place == 0, pair(0, 2 * STEPS + 2), jnp.where(place == 1, own_lon, pair(1, 2 * STEPS + 2)))
         lat_gap = jnp.abs(lat + (place - 1).astype(F32) * rows - cell_row) * (1.0 / rows)
         lon_gap = jnp.abs(jnp.broadcast_to(east, cell_lon.shape) - cell_lon)
         lon_gap = jnp.minimum(lon_gap, lon - lon_gap) * (4.0 / lon)
@@ -256,41 +260,43 @@
 
 
 def transform(
-    listed_ref, columns_ref, weight_hbm, own_ref, fetched_ref, swapped_ref, analysed_ref,
-    observed_ref, weight_ref, series_ref, scaled_ref, combined_ref, sems,
+    listed_ref, columns_ref, weight_ref, own_ref, fetched_ref, swapped_hbm, analysed_ref,
+    observed_ref, series_ref, scaled_ref, combined_ref, sems,
 ):
     shares, share, cells = columns_ref.shape
     obs_rows = own_ref.shape[1]
     first_core = lax.rem(lax.axis_index("mem"), 2) == 0
-    copies = []
-    for position in range(LIST):
-        target = observed_ref.at[pl.ds(position * obs_rows, obs_rows), :]
+    blocks = [slice(position * obs_rows, (position + 1) * obs_rows) for position in range(LIST)]
+    halves = [slice(half * obs_rows, (half + 1) * obs_rows) for half in range(shares * share // obs_rows)]
+
+    def take(source_ref, block):
+        def copy():
+            observed_ref[block, :] = source_ref[0]
+
+        return copy
+
+    waits = []
+    for position, block in enumerate(blocks):
         place = place_of(listed_ref, position)
-        near = place != 1
-        fetched = jnp.logical_and(near, (place == 0) == first_core)
-        swapped = jnp.logical_and(near, (place == 0) != first_core)
-        for chosen, source in ((place == 1, own_ref), (fetched, fetched_ref), (swapped, swapped_ref)):
-            copy = pltpu.make_async_copy(source.at[0], target, sems.at[position])
-            pl.when(chosen)(copy.start)
-        copies.append(copy)
-        if position == 0:
-            weight_copy = pltpu.make_async_copy(weight_hbm, weight_ref, sems.at[LIST])
-            weight_copy.start()
+        swapped = jnp.logical_and(place != 1, (place == 0) != first_core)
+        copy = pltpu.make_async_copy(swapped_hbm.at[0], observed_ref.at[block, :], sems.at[position])
+        pl.when(swapped)(copy.start)
+        waits.append((swapped, copy.wait))
+    for position, block in enumerate(blocks):
+        place = place_of(listed_ref, position)
+        pl.when(place == 1)(take(own_ref, block))
+        pl.when(jnp.logical_and(place != 1, (place == 0) == first_core))(take(fetched_ref, block))
     columns = jnp.transpose(columns_ref[...].reshape(shares * share, cells)) * (1.0 / SEND_SCALE)
     average = jnp.mean(columns, axis=1, keepdims=True)
     series_ref[...] = (columns - average).astype(BF16)
     combined_ref[...] = columns
-    blocks = [slice(position * obs_rows, (position + 1) * obs_rows) for position in range(LIST)]
-    halves = [slice(half * obs_rows, (half + 1) * obs_rows) for half in range(shares * share // obs_rows)]
     for power in range(1, DEGREE + 1):
-        for position, block in enumerate(blocks):
+        for (swapped, wait), block in zip(waits, blocks):
             if power == 1:
-                copies[position].wait()
+                pl.when(swapped)(wait)
             projected = lax.dot_general(
                 series_ref[...], observed_ref[block, :], (((1,), (1,)), ((), ())), preferred_element_type=F32
             )
-            if power == 1 and position == 0:
-                weight_copy.wait()
             scaled_ref[:, block] = (projected * weight_ref[:, block]).astype(BF16)
         for half in halves:
             series = jnp.dot(scaled_ref[...], observed_ref[:, half], preferred_element_type=F32)
@@ -315,7 +321,7 @@
     shares = lax.axis_size("mem")
     obs_rows, all_members = obs_pert.shape[1:]
     cells = rows * lon // shares
-    message = pltpu.VMEM((STEPS, members + EXTRA, lon), BF16)
+    message = pltpu.VMEM((STEPS * members + EXTRA, lon), BF16)
     halo_scratch = [pltpu.VMEM((STEPS, members, lon), F32), pltpu.VMEM((STEPS, 4, 8, lon), F32)]
     ring = [
         (band * shares + mem, (band + (-1 if mem % 2 else 1)) % bands * shares + mem)
@@ -336,7 +342,7 @@
             pltpu.VMEM((members * rows * lon // LANES, LANES), F32),
             pltpu.VMEM(courant.shape, F32),
             pltpu.VMEM(obs_cell.shape, jnp.int32),
-            pltpu.SemaphoreType.DMA((3,)),
+            pltpu.SemaphoreType.DMA((PIECES + 2,)),
         ],
         compiler_params=PARAMS,
         name="pack",
@@ -386,7 +392,7 @@
     swapped = lax.ppermute(held, "mem", [(mem, mem ^ 1) for mem in range(shares)])
     weight = pl.pallas_call(
         functools.partial(localize, rows, lon, 1.0 / (all_members + LIST * obs_rows)),
-        out_shape=jax.ShapeDtypeStruct((cells, LIST * obs_rows), F32),
+        out_shape=pltpu.VMEM((cells, LIST * obs_rows), F32),
         in_specs=[SMEM, SMEM, VMEM, VMEM],
         out_specs=VMEM,
         compiler_params=PARAMS,
@@ -395,19 +401,18 @@
     analysed = pl.pallas_call(
         transform,
         out_shape=pltpu.VMEM((shares, members, cells), BF16),
-        in_specs=[SMEM, VMEM, ANY, ANY, ANY, ANY],
+        in_specs=[SMEM] + [VMEM] * 4 + [HBM],
         out_specs=VMEM,
         scratch_shapes=[
             pltpu.VMEM((LIST * obs_rows, all_members), BF16),
-            pltpu.VMEM((cells, LIST * obs_rows), F32),
             pltpu.VMEM((cells, all_members), BF16),
             pltpu.VMEM((cells, LIST * obs_rows), BF16),
             pltpu.VMEM((cells, all_members), F32),
-            pltpu.SemaphoreType.DMA((LIST + 1,)),
+            pltpu.SemaphoreType.DMA((LIST,)),
         ],
         compiler_params=PARAMS,
         name="transform",
-    )(band_list, in_vmem(columns), weight, obs_pert, fetched, swapped)
+    )(band_list, *[in_vmem(x) for x in (columns, weight, obs_pert, fetched)], in_hbm(swapped))
     returned = lax.all_to_all(analysed, "mem", split_axis=0, concat_axis=0, tiled=True)
     out = pl.pallas_call(
         functools.partial(unpack, members, rows),

time: 90.2 us -> 89.7 us (level)
  transfers between devices with their start and end apart: 5 -> 5, of which waited for: 3 -> 3; matrix products, arithmetic and copies ran while one was open for 1% -> 1% of each run, Pallas kernels for 6% -> 7%
where the time goes in v4:
time: 89.7 us; the launch traced here: 89.3 us
  starting transfers between devices  43.1 us (48%)
  waiting for transfers between devices  15.4 us (17%)
  Pallas kernels  15.2 us (17%)
  blocking collectives  14.1 us (16%)
    ppermute x1, starting transfers between devices, shards(): fetched = lax.ppermute(source, ('band', 'mem'), ring)  21 us
    all_to_all x1, blocking collectives, shards(): lax.all_to_all(analysed, 'mem', split_axis=0, concat_axis=0, tiled=True)  14.1 us
    all_to_all x1, waiting for transfers between devices, shards(): lax.all_to_all(groups.astype(jnp.float16), 'mem', split_axis=0, concat_ax...  10.1 us
    all_to_all x1, starting transfers between devices, shards(): lax.all_to_all(groups.astype(jnp.float16), 'mem', split_axis=0, concat_ax...  7.36 us
    ppermute x1, starting transfers between devices, shards(): lax.ppermute(northward, 'band', [((band + 1) % bands, band) for band in r...  6.68 us
    ppermute x1, starting transfers between devices, shards(): lax.ppermute(held, 'mem', [(mem, mem ^ 1) for mem in range(shares)])  6.16 us
    pallas_call x1, Pallas kernels, shards(): pl.pallas_call(transform, out_shape=pltpu.VMEM((shares, members, cells),...  6.1 us
    ppermute x1, waiting for transfers between devices, shards(): lax.ppermute(southward, 'band', [(band, (band + 1) % bands) for band in r...  3.69 us
  transfers between devices with their start and end apart: 5, of which 3 were waited for; matrix products, arithmetic and copies ran while one was open for 1% of the time, Pallas kernels for 7%

profile of v4, /device:TPU:1, one launch (start us, length us, event | category | flops | bytes accessed | tf_op | source)
XLA Modules:
  0.0 89.3 jit_solution(17548337149100386702)
XLA Ops:
  0.0 0.0 copy-start
  0.0 1.3 %pack.1 = (bf16[400,256]{1,0:T(8,128)(2,1)S(1)}, bf16[400,256]{1,0:T(8,128)(2,1)S(1)}, f32[8,64,256]{2,1,0:T(8,128)S(1)}, f32[8,4,8,256]{3,2,1,0:T(8,128)S(1)}) custom-call(f32[1024,128]{1,0:T(8,128)} %bitcast.10, f32[2,8,256]{2,1,0:T(8,128)} %courant_hbm.1, s32[1,512]{1,0:T(1,128)} %cells_ref.1), custom_call_target="tpu_custom_call" | custom-call | tf_op jit(solution)/shard_map/pack/pallas_call | solution.py:331
  1.3 0.9 %inner.1.inner_ref = f32[10,64,256]{2,1,0:T(8,128)S(1)} custom-call(f32[8,64,256]{2,1,0:T(8,128)S(1)} %get-tuple-element.13.fields_ref, f32[8,4,8,256]{3,2,1,0:T(8,128)S(1)} %get-tuple-element.14.winds_ref), custom_call_target="tpu_custom_call" | custom-call | tf_op jit(solution)/shard_map/inner/pallas_call | solution.py:357
  2.3 0.0 copy-done
  2.3 21.0 %collective-permute-start.2 = (bf16[1,512,1024]{2,1,0:T(8,128)(2,1)S(1)}, bf16[1,512,1024]{2,1,0:T(8,128)(2,1)S(1)}, u32[]{:S(2)}, u32[]{:S(2)}) collective-permute-start(bf16[1,512,1024]{2,1,0:T(8,128)(2,1)S(1)} %copy-done), channel_id=1, source_target_pairs={{0,16},{1,1009},{2,18},{3,1011},{4,20},{5,1013},{6,22},{7,1015},{8... | collective-permute-start | bytes 3145736 | tf_op jit(solution)/shard_map/ppermute | solution.py:366
  23.2 1.9 %collective-permute-start = (bf16[400,256]{1,0:T(8,128)(2,1)S(1)}, bf16[400,256]{1,0:T(8,128)(2,1)S(1)}, u32[]{:S(2)}, u32[]{:S(2)}) collective-permute-start(bf16[400,256]{1,0:T(8,128)(2,1)S(1)} %get-tuple-element.15), channel_id=1, source_target_pairs={{0,16},{16,32},{32,48},{48,64},{64,80},{80,96},{96,112},{112,128},... | collective-permute-start | bytes 614408 | tf_op jit(solution)/shard_map/ppermute | solution.py:354
  25.2 6.7 %collective-permute-start.1 = (bf16[400,256]{1,0:T(8,128)(2,1)S(1)}, bf16[400,256]{1,0:T(8,128)(2,1)S(1)}, u32[]{:S(2)}, u32[]{:S(2)}) collective-permute-start(bf16[400,256]{1,0:T(8,128)(2,1)S(1)} %get-tuple-element.16), channel_id=1, source_target_pairs={{16,0},{32,16},{48,32},{64,48},{80,64},{96,80},{112,96},{128,112},... | collective-permute-start | bytes 614408 | tf_op jit(solution)/shard_map/ppermute | solution.py:355
  31.9 3.7 %collective-permute-done.message_ref.above_ref = bf16[400,256]{1,0:T(8,128)(2,1)S(1)} collective-permute-done((bf16[400,256]{1,0:T(8,128)(2,1)S(1)}, bf16[400,256]{1,0:T(8,128)(2,1)S(1)}, u32[]{:S(2)}, u32[]{:S(2)}) %collective-permute-start) | collective-permute-done | bytes 204832 | tf_op jit(solution)/shard_map/ppermute | solution.py:354
  35.5 2.2 %upper.1.upper_ref = f32[6,64,256]{2,1,0:T(8,128)S(1)} custom-call(f32[8,64,256]{2,1,0:T(8,128)S(1)} %get-tuple-element.13.fields_ref, f32[8,4,8,256]{3,2,1,0:T(8,128)S(1)} %get-tuple-element.14.winds_ref, f32[10,64,256]{2,1,0:T(8,128)S(1)} %inner.1.inner_ref, bf16[400,256]{1,0:T(8,128)(2,1)S(1)} %collective-permute-done.message_ref.above_ref), custom_call_target="tpu_custom_call" | custom-call | tf_op jit(solution)/shard_map/upper/pallas_call | solution.py:368
  37.8 1.6 %collective-permute-done.1.message_ref = bf16[400,256]{1,0:T(8,128)(2,1)S(1)} collective-permute-done((bf16[400,256]{1,0:T(8,128)(2,1)S(1)}, bf16[400,256]{1,0:T(8,128)(2,1)S(1)}, u32[]{:S(2)}, u32[]{:S(2)}) %collective-permute-start.1) | collective-permute-done | bytes 204832 | tf_op jit(solution)/shard_map/ppermute | solution.py:355
  39.4 2.8 %lower.1 = (f32[16,64,128]{2,1,0:T(8,128)S(1)}, f32[2,16,256]{2,1,0:T(8,128)S(1)}) custom-call(f32[8,64,256]{2,1,0:T(8,128)S(1)} %get-tuple-element.13.fields_ref, f32[8,4,8,256]{3,2,1,0:T(8,128)S(1)} %get-tuple-element.14.winds_ref, f32[10,64,256]{2,1,0:T(8,128)S(1)} %inner.1.inner_ref, f32[6,64,256]{2,1,0:T(8,128)S(1)} %upper.1.upper_ref, ...), custom_call_target="tpu_custom_call" | custom-call | tf_op jit(solution)/shard_map/lower/pallas_call | solution.py:377
  42.2 0.0 collective-permute-done.2.fetched_ref
  42.2 6.2 %collective-permute-start.3 = (bf16[1,512,1024]{2,1,0:T(8,128)(2,1)S(1)}, bf16[1,512,1024]{2,1,0:T(8,128)(2,1)}, u32[]{:S(2)}, u32[]{:S(2)}) collective-permute-start(bf16[1,512,1024]{2,1,0:T(8,128)(2,1)S(1)} %collective-permute-done.2.fetched_ref), channel_id=1, source_target_pairs={{0,1},{1,0},{2,3},{3,2},{4,5},{5,4},{6,7},{7,6},{8,9},{9,8},{10,11... | collective-permute-start | bytes 3145736 | tf_op jit(solution)/shard_map/ppermute | solution.py:392
  48.3 0.8 convert_element_type.6
  49.1 0.0 copy-start.1
  49.1 7.4 %all-to-all-start = ((f16[16,64,128]{2,1,0:T(8,128)(2,1)}), f16[16,64,128]{2,1,0:T(8,128)(2,1)S(1)}, u32[]{:S(2)}, u32[]{:S(2)}) async-start(f16[16,64,128]{2,1,0:T(8,128)(2,1)} %convert_element_type.6), calls=%async_computation | async-start | bytes 524288 | tf_op jit(solution)/shard_map/all_to_all | solution.py:389
  56.4 0.0 copy-start.2
  56.5 0.0 copy-start.3
  56.5 0.0 copy-done.1
  56.5 0.6 copy-done.2
  57.1 0.0 copy-done.3
  57.1 0.8 localize.1.weight_ref
  57.9 10.1 %all-to-all-done = f16[16,64,128]{2,1,0:T(8,128)(2,1)S(1)} async-done(((f16[16,64,128]{2,1,0:T(8,128)(2,1)}), f16[16,64,128]{2,1,0:T(8,128)(2,1)S(1)}, u32[]{:S(2)}, u32[]{:S(2)}) %all-to-all-start) | async-done | bytes 262176 | tf_op jit(solution)/shard_map/all_to_all | solution.py:389
  68.1 0.0 collective-permute-done.3.swapped_hbm
  68.1 6.1 %transform.1 = bf16[16,64,128]{2,1,0:T(8,128)(2,1)S(1)} custom-call(s32[1,2]{1,0:T(1,128)S(1)} %copy-done.2, f32[16,64,128]{2,1,0:T(8,128)S(1)} %convert_element_type.7.columns_ref, f32[128,1024]{1,0:T(8,128)S(1)} %localize.1.weight_ref, bf16[1,512,1024]{2,1,0:T(8,128)(2,1)S(1)} %copy-done, bf16[1,512,1024]{2,1,0:T(8,128)(2,1)S(1)} %collective-permute-done.2.fetched_ref, ...), custom_call_target="tpu_custom_call" | custom-call | tf_op jit(solution)/shard_map/transform/pallas_call | solution.py:401
  74.2 14.1 %all_to_all.10.returned_ref = bf16[16,64,128]{2,1,0:T(8,128)(2,1)S(1)} all-to-all(bf16[16,64,128]{2,1,0:T(8,128)(2,1)S(1)} %transform.1), channel_id=1, replica_groups=mesh['band'=64,'mem'=16] {'mem'}, dimensions={0} | all-to-all | bytes 524288 | tf_op jit(solution)/shard_map/all_to_all | solution.py:416
  88.3 1.0 %unpack.1 = f32[1024,128]{1,0:T(8,128)} custom-call(bf16[16,64,128]{2,1,0:T(8,128)(2,1)S(1)} %all_to_all.10.returned_ref), custom_call_target="tpu_custom_call" | custom-call | tf_op jit(solution)/shard_map/unpack/pallas_call | solution.py:417
  (1 shorter events, 0.0 us)
Async XLA Ops:
  0.0 2.3 %copy-start = (bf16[1,512,1024]{2,1,0:T(8,128)(2,1)S(1)}, bf16[1,512,1024]{2,1,0:T(8,128)(2,1)}, u32[]{:S(2)}) copy-start(bf16[1,512,1024]{2,1,0:T(8,128)(2,1)} %own_ref.1) | copy-start | bytes 3145732
  2.3 39.9 %collective-permute-start.2 = (bf16[1,512,1024]{2,1,0:T(8,128)(2,1)S(1)}, bf16[1,512,1024]{2,1,0:T(8,128)(2,1)S(1)}, u32[]{:S(2)}, u32[]{:S(2)}) collective-permute-start(bf16[1,512,1024]{2,1,0:T(8,128)(2,1)S(1)} %copy-done), channel_id=1, source_target_pairs={{0,16},{1,1009},{2,18},{3,1011},{4,20},{5,1013},{6,22},{7,1015},{8... | collective-permute-start | bytes 3145736 | tf_op jit(solution)/shard_map/ppermute | solution.py:366
  23.2 12.3 %collective-permute-start = (bf16[400,256]{1,0:T(8,128)(2,1)S(1)}, bf16[400,256]{1,0:T(8,128)(2,1)S(1)}, u32[]{:S(2)}, u32[]{:S(2)}) collective-permute-start(bf16[400,256]{1,0:T(8,128)(2,1)S(1)} %get-tuple-element.15), channel_id=1, source_target_pairs={{0,16},{16,32},{32,48},{48,64},{64,80},{80,96},{96,112},{112,128},... | collective-permute-start | bytes 614408 | tf_op jit(solution)/shard_map/ppermute | solution.py:354
  25.2 14.2 %collective-permute-start.1 = (bf16[400,256]{1,0:T(8,128)(2,1)S(1)}, bf16[400,256]{1,0:T(8,128)(2,1)S(1)}, u32[]{:S(2)}, u32[]{:S(2)}) collective-permute-start(bf16[400,256]{1,0:T(8,128)(2,1)S(1)} %get-tuple-element.16), channel_id=1, source_target_pairs={{16,0},{32,16},{48,32},{64,48},{80,64},{96,80},{112,96},{128,112},... | collective-permute-start | bytes 614408 | tf_op jit(solution)/shard_map/ppermute | solution.py:355
  42.2 25.9 %collective-permute-start.3 = (bf16[1,512,1024]{2,1,0:T(8,128)(2,1)S(1)}, bf16[1,512,1024]{2,1,0:T(8,128)(2,1)}, u32[]{:S(2)}, u32[]{:S(2)}) collective-permute-start(bf16[1,512,1024]{2,1,0:T(8,128)(2,1)S(1)} %collective-permute-done.2.fetched_ref), channel_id=1, source_target_pairs={{0,1},{1,0},{2,3},{3,2},{4,5},{5,4},{6,7},{7,6},{8,9},{9,8},{10,11... | collective-permute-start | bytes 3145736 | tf_op jit(solution)/shard_map/ppermute | solution.py:392
  49.1 7.4 %copy-start.1 = (s32[1,512]{1,0:T(1,128)S(1)}, s32[1,512]{1,0:T(1,128)}, u32[]{:S(2)}) copy-start(s32[1,512]{1,0:T(1,128)} %cells_ref.1) | copy-start | bytes 6148
  49.1 18.9 %all-to-all-start = ((f16[16,64,128]{2,1,0:T(8,128)(2,1)}), f16[16,64,128]{2,1,0:T(8,128)(2,1)S(1)}, u32[]{:S(2)}, u32[]{:S(2)}) async-start(f16[16,64,128]{2,1,0:T(8,128)(2,1)} %convert_element_type.6), calls=%async_computation | async-start | bytes 524288 | tf_op jit(solution)/shard_map/all_to_all | solution.py:389
  56.4 0.7 copy-start.2
  56.5 0.7 copy-start.3

commit v5 on v4

--- a/solution.py
+++ b/solution.py
@@ -309,10 +309,22 @@
                 analysed_ref[first:last] = jnp.transpose(combined.astype(BF16)).reshape(last - first, share, cells)
 
 
-def unpack(members, rows, returned_ref, out_ref):
-    for row in range(rows):
-        for side in range(2):
-            out_ref[pl.ds(side * rows + row, members, stride=2 * rows), :] = returned_ref[2 * row + side].astype(F32)
+def unpack(members, rows, returned_ref, out_hbm, out_ref, sems):
+    share = members // PIECES
+    length = out_ref.shape[0] // PIECES
+    copies = []
+    for piece in range(PIECES):
+        first = piece * share
+        for row in range(rows):
+            for side in range(2):
+                out_ref[pl.ds((first * 2 + side) * rows + row, share, stride=2 * rows), :] = returned_ref[
+                    2 * row + side, first : first + share, :
+                ].astype(F32)
+        part = pl.ds(piece * length, length)
+        copies.append(pltpu.make_async_copy(out_ref.at[part], out_hbm.at[part], sems.at[piece]))
+        copies[-1].start()
+    for copy in copies:
+        copy.wait()
 
 
 def shards(state, courant, obs_pert, obs_cell, block_rows, band_list):
@@ -418,7 +430,11 @@
         functools.partial(unpack, members, rows),
         out_shape=jax.ShapeDtypeStruct((members * 2 * rows, LANES), F32),
         in_specs=[VMEM],
-        out_specs=VMEM,
+        out_specs=HBM,
+        scratch_shapes=[
+            pltpu.VMEM((members * 2 * rows, LANES), F32),
+            pltpu.SemaphoreType.DMA((PIECES,)),
+        ],
         compiler_params=pltpu.CompilerParams(vmem_limit_bytes=16 << 20),
         name="unpack",
     )(in_vmem(returned))

time: 89.7 us -> 89.6 us (level)
  no operation moved by 1% of the time
where the time goes in v5:
time: 89.6 us; the launch traced here: 89.1 us
  starting transfers between devices  43.1 us (48%)
  waiting for transfers between devices  15.4 us (17%)
  Pallas kernels  15 us (17%)
  blocking collectives  14.1 us (16%)
    ppermute x1, starting transfers between devices, shards(): fetched = lax.ppermute(source, ('band', 'mem'), ring)  21 us
    all_to_all x1, blocking collectives, shards(): lax.all_to_all(analysed, 'mem', split_axis=0, concat_axis=0, tiled=True)  14.1 us
    all_to_all x1, waiting for transfers between devices, shards(): lax.all_to_all(groups.astype(jnp.float16), 'mem', split_axis=0, concat_ax...  10.1 us
    all_to_all x1, starting transfers between devices, shards(): lax.all_to_all(groups.astype(jnp.float16), 'mem', split_axis=0, concat_ax...  7.36 us
    ppermute x1, starting transfers between devices, shards(): lax.ppermute(northward, 'band', [((band + 1) % bands, band) for band in r...  6.68 us
    ppermute x1, starting transfers between devices, shards(): lax.ppermute(held, 'mem', [(mem, mem ^ 1) for mem in range(shares)])  6.16 us
    pallas_call x1, Pallas kernels, shards(): pl.pallas_call(transform, out_shape=pltpu.VMEM((shares, members, cells),...  6.1 us
    ppermute x1, waiting for transfers between devices, shards(): lax.ppermute(southward, 'band', [(band, (band + 1) % bands) for band in r...  3.69 us
  transfers between devices with their start and end apart: 5, of which 3 were waited for; matrix products, arithmetic and copies ran while one was open for 1% of the time, Pallas kernels for 7%

profile of v5, /device:TPU:1, one launch (start us, length us, event | category | flops | bytes accessed | tf_op | source)
XLA Modules:
  0.0 89.1 jit_solution(4192746532155703827)
XLA Ops:
  0.0 0.0 copy-start
  0.0 1.3 %pack.1 = (bf16[400,256]{1,0:T(8,128)(2,1)S(1)}, bf16[400,256]{1,0:T(8,128)(2,1)S(1)}, f32[8,64,256]{2,1,0:T(8,128)S(1)}, f32[8,4,8,256]{3,2,1,0:T(8,128)S(1)}) custom-call(f32[1024,128]{1,0:T(8,128)} %bitcast.10, f32[2,8,256]{2,1,0:T(8,128)} %courant_hbm.1, s32[1,512]{1,0:T(1,128)} %cells_ref.1), custom_call_target="tpu_custom_call" | custom-call | tf_op jit(solution)/shard_map/pack/pallas_call | solution.py:343
  1.3 0.9 %inner.1.inner_ref = f32[10,64,256]{2,1,0:T(8,128)S(1)} custom-call(f32[8,64,256]{2,1,0:T(8,128)S(1)} %get-tuple-element.13.fields_ref, f32[8,4,8,256]{3,2,1,0:T(8,128)S(1)} %get-tuple-element.14.winds_ref), custom_call_target="tpu_custom_call" | custom-call | tf_op jit(solution)/shard_map/inner/pallas_call | solution.py:369
  2.3 0.0 copy-done
  2.3 21.0 %collective-permute-start.2 = (bf16[1,512,1024]{2,1,0:T(8,128)(2,1)S(1)}, bf16[1,512,1024]{2,1,0:T(8,128)(2,1)S(1)}, u32[]{:S(2)}, u32[]{:S(2)}) collective-permute-start(bf16[1,512,1024]{2,1,0:T(8,128)(2,1)S(1)} %copy-done), channel_id=1, source_target_pairs={{0,16},{1,1009},{2,18},{3,1011},{4,20},{5,1013},{6,22},{7,1015},{8... | collective-permute-start | bytes 3145736 | tf_op jit(solution)/shard_map/ppermute | solution.py:378
  23.2 1.9 %collective-permute-start = (bf16[400,256]{1,0:T(8,128)(2,1)S(1)}, bf16[400,256]{1,0:T(8,128)(2,1)S(1)}, u32[]{:S(2)}, u32[]{:S(2)}) collective-permute-start(bf16[400,256]{1,0:T(8,128)(2,1)S(1)} %get-tuple-element.15), channel_id=1, source_target_pairs={{0,16},{16,32},{32,48},{48,64},{64,80},{80,96},{96,112},{112,128},... | collective-permute-start | bytes 614408 | tf_op jit(solution)/shard_map/ppermute | solution.py:366
  25.2 6.7 %collective-permute-start.1 = (bf16[400,256]{1,0:T(8,128)(2,1)S(1)}, bf16[400,256]{1,0:T(8,128)(2,1)S(1)}, u32[]{:S(2)}, u32[]{:S(2)}) collective-permute-start(bf16[400,256]{1,0:T(8,128)(2,1)S(1)} %get-tuple-element.16), channel_id=1, source_target_pairs={{16,0},{32,16},{48,32},{64,48},{80,64},{96,80},{112,96},{128,112},... | collective-permute-start | bytes 614408 | tf_op jit(solution)/shard_map/ppermute | solution.py:367
  31.9 3.7 %collective-permute-done.message_ref.above_ref = bf16[400,256]{1,0:T(8,128)(2,1)S(1)} collective-permute-done((bf16[400,256]{1,0:T(8,128)(2,1)S(1)}, bf16[400,256]{1,0:T(8,128)(2,1)S(1)}, u32[]{:S(2)}, u32[]{:S(2)}) %collective-permute-start) | collective-permute-done | bytes 204832 | tf_op jit(solution)/shard_map/ppermute | solution.py:366
  35.5 2.2 %upper.1.upper_ref = f32[6,64,256]{2,1,0:T(8,128)S(1)} custom-call(f32[8,64,256]{2,1,0:T(8,128)S(1)} %get-tuple-element.13.fields_ref, f32[8,4,8,256]{3,2,1,0:T(8,128)S(1)} %get-tuple-element.14.winds_ref, f32[10,64,256]{2,1,0:T(8,128)S(1)} %inner.1.inner_ref, bf16[400,256]{1,0:T(8,128)(2,1)S(1)} %collective-permute-done.message_ref.above_ref), custom_call_target="tpu_custom_call" | custom-call | tf_op jit(solution)/shard_map/upper/pallas_call | solution.py:380
  37.8 1.6 %collective-permute-done.1.message_ref = bf16[400,256]{1,0:T(8,128)(2,1)S(1)} collective-permute-done((bf16[400,256]{1,0:T(8,128)(2,1)S(1)}, bf16[400,256]{1,0:T(8,128)(2,1)S(1)}, u32[]{:S(2)}, u32[]{:S(2)}) %collective-permute-start.1) | collective-permute-done | bytes 204832 | tf_op jit(solution)/shard_map/ppermute | solution.py:367
  39.4 2.8 %lower.1 = (f32[16,64,128]{2,1,0:T(8,128)S(1)}, f32[2,16,256]{2,1,0:T(8,128)S(1)}) custom-call(f32[8,64,256]{2,1,0:T(8,128)S(1)} %get-tuple-element.13.fields_ref, f32[8,4,8,256]{3,2,1,0:T(8,128)S(1)} %get-tuple-element.14.winds_ref, f32[10,64,256]{2,1,0:T(8,128)S(1)} %inner.1.inner_ref, f32[6,64,256]{2,1,0:T(8,128)S(1)} %upper.1.upper_ref, ...), custom_call_target="tpu_custom_call" | custom-call | tf_op jit(solution)/shard_map/lower/pallas_call | solution.py:389
  42.2 0.0 collective-permute-done.2.fetched_ref
  42.2 6.2 %collective-permute-start.3 = (bf16[1,512,1024]{2,1,0:T(8,128)(2,1)S(1)}, bf16[1,512,1024]{2,1,0:T(8,128)(2,1)}, u32[]{:S(2)}, u32[]{:S(2)}) collective-permute-start(bf16[1,512,1024]{2,1,0:T(8,128)(2,1)S(1)} %collective-permute-done.2.fetched_ref), channel_id=1, source_target_pairs={{0,1},{1,0},{2,3},{3,2},{4,5},{5,4},{6,7},{7,6},{8,9},{9,8},{10,11... | collective-permute-start | bytes 3145736 | tf_op jit(solution)/shard_map/ppermute | solution.py:404
  48.3 0.8 convert_element_type.6
  49.1 0.0 copy-start.1
  49.1 7.4 %all-to-all-start = ((f16[16,64,128]{2,1,0:T(8,128)(2,1)}), f16[16,64,128]{2,1,0:T(8,128)(2,1)S(1)}, u32[]{:S(2)}, u32[]{:S(2)}) async-start(f16[16,64,128]{2,1,0:T(8,128)(2,1)} %convert_element_type.6), calls=%async_computation | async-start | bytes 524288 | tf_op jit(solution)/shard_map/all_to_all | solution.py:401
  56.4 0.0 copy-start.2
  56.5 0.0 copy-start.3
  56.5 0.0 copy-done.1
  56.5 0.6 copy-done.2
  57.1 0.0 copy-done.3
  57.1 0.8 localize.1.weight_ref
  57.9 10.1 %all-to-all-done = f16[16,64,128]{2,1,0:T(8,128)(2,1)S(1)} async-done(((f16[16,64,128]{2,1,0:T(8,128)(2,1)}), f16[16,64,128]{2,1,0:T(8,128)(2,1)S(1)}, u32[]{:S(2)}, u32[]{:S(2)}) %all-to-all-start) | async-done | bytes 262176 | tf_op jit(solution)/shard_map/all_to_all | solution.py:401
  68.1 0.0 collective-permute-done.3.swapped_hbm
  68.1 6.1 %transform.1 = bf16[16,64,128]{2,1,0:T(8,128)(2,1)S(1)} custom-call(s32[1,2]{1,0:T(1,128)S(1)} %copy-done.2, f32[16,64,128]{2,1,0:T(8,128)S(1)} %convert_element_type.7.columns_ref, f32[128,1024]{1,0:T(8,128)S(1)} %localize.1.weight_ref, bf16[1,512,1024]{2,1,0:T(8,128)(2,1)S(1)} %copy-done, bf16[1,512,1024]{2,1,0:T(8,128)(2,1)S(1)} %collective-permute-done.2.fetched_ref, ...), custom_call_target="tpu_custom_call" | custom-call | tf_op jit(solution)/shard_map/transform/pallas_call | solution.py:413
  74.2 14.1 %all_to_all.10.returned_ref = bf16[16,64,128]{2,1,0:T(8,128)(2,1)S(1)} all-to-all(bf16[16,64,128]{2,1,0:T(8,128)(2,1)S(1)} %transform.1), channel_id=1, replica_groups=mesh['band'=64,'mem'=16] {'mem'}, dimensions={0} | all-to-all | bytes 524288 | tf_op jit(solution)/shard_map/all_to_all | solution.py:428
  88.3 0.9 unpack.1
  (1 shorter events, 0.0 us)
Async XLA Ops:
  0.0 2.3 %copy-start = (bf16[1,512,1024]{2,1,0:T(8,128)(2,1)S(1)}, bf16[1,512,1024]{2,1,0:T(8,128)(2,1)}, u32[]{:S(2)}) copy-start(bf16[1,512,1024]{2,1,0:T(8,128)(2,1)} %own_ref.1) | copy-start | bytes 3145732
  2.3 39.9 %collective-permute-start.2 = (bf16[1,512,1024]{2,1,0:T(8,128)(2,1)S(1)}, bf16[1,512,1024]{2,1,0:T(8,128)(2,1)S(1)}, u32[]{:S(2)}, u32[]{:S(2)}) collective-permute-start(bf16[1,512,1024]{2,1,0:T(8,128)(2,1)S(1)} %copy-done), channel_id=1, source_target_pairs={{0,16},{1,1009},{2,18},{3,1011},{4,20},{5,1013},{6,22},{7,1015},{8... | collective-permute-start | bytes 3145736 | tf_op jit(solution)/shard_map/ppermute | solution.py:378
  23.2 12.3 %collective-permute-start = (bf16[400,256]{1,0:T(8,128)(2,1)S(1)}, bf16[400,256]{1,0:T(8,128)(2,1)S(1)}, u32[]{:S(2)}, u32[]{:S(2)}) collective-permute-start(bf16[400,256]{1,0:T(8,128)(2,1)S(1)} %get-tuple-element.15), channel_id=1, source_target_pairs={{0,16},{16,32},{32,48},{48,64},{64,80},{80,96},{96,112},{112,128},... | collective-permute-start | bytes 614408 | tf_op jit(solution)/shard_map/ppermute | solution.py:366
  25.2 14.2 %collective-permute-start.1 = (bf16[400,256]{1,0:T(8,128)(2,1)S(1)}, bf16[400,256]{1,0:T(8,128)(2,1)S(1)}, u32[]{:S(2)}, u32[]{:S(2)}) collective-permute-start(bf16[400,256]{1,0:T(8,128)(2,1)S(1)} %get-tuple-element.16), channel_id=1, source_target_pairs={{16,0},{32,16},{48,32},{64,48},{80,64},{96,80},{112,96},{128,112},... | collective-permute-start | bytes 614408 | tf_op jit(solution)/shard_map/ppermute | solution.py:367
  42.2 25.9 %collective-permute-start.3 = (bf16[1,512,1024]{2,1,0:T(8,128)(2,1)S(1)}, bf16[1,512,1024]{2,1,0:T(8,128)(2,1)}, u32[]{:S(2)}, u32[]{:S(2)}) collective-permute-start(bf16[1,512,1024]{2,1,0:T(8,128)(2,1)S(1)} %collective-permute-done.2.fetched_ref), channel_id=1, source_target_pairs={{0,1},{1,0},{2,3},{3,2},{4,5},{5,4},{6,7},{7,6},{8,9},{9,8},{10,11... | collective-permute-start | bytes 3145736 | tf_op jit(solution)/shard_map/ppermute | solution.py:404
  49.1 7.4 %copy-start.1 = (s32[1,512]{1,0:T(1,128)S(1)}, s32[1,512]{1,0:T(1,128)}, u32[]{:S(2)}) copy-start(s32[1,512]{1,0:T(1,128)} %cells_ref.1) | copy-start | bytes 6148
  49.1 18.9 %all-to-all-start = ((f16[16,64,128]{2,1,0:T(8,128)(2,1)}), f16[16,64,128]{2,1,0:T(8,128)(2,1)S(1)}, u32[]{:S(2)}, u32[]{:S(2)}) async-start(f16[16,64,128]{2,1,0:T(8,128)(2,1)} %convert_element_type.6), calls=%async_computation | async-start | bytes 524288 | tf_op jit(solution)/shard_map/all_to_all | solution.py:401
  56.4 0.7 copy-start.2
  56.5 0.7 copy-start.3
